TPU v7x, 768 devices: a whole 4x8x12 slice. The times are simulated.
768 devices in a mesh: region: 64 (over x, y, core), dom: 12 (over z).
Axes of the slice: x: 4, y: 8, z: 12, core: 2. Of those that a mesh axis runs over, the one named last changes fastest.
Arguments:
- water_state: float32 [3, 10, 393216], P(None, None, ('region', 'dom')), may hold values from -6 to 6
- water_depth: float32 [393216], P(('region', 'dom')), may hold values from 0.3 to 3
- metric: float32 [4, 393216], P(None, ('region', 'dom'))
- diff_ops: float32 [2, 10, 10], replicated, may hold values from -2 to 2
- stiff_ops: float32 [2, 10, 10], replicated, may hold values from -2 to 2
- trace_ops: float32 [3, 4, 10], replicated, may hold values from -2 to 2
- lift_ops: float32 [3, 10, 4], replicated, may hold values from -3 to 3
- cluster: int32 [393216], P(('region', 'dom')), may hold values from 0 to 1, as said below
- face_code: int32 [3, 393216], P(None, ('region', 'dom')), may hold values from 0 to 2304, as said below
- send_region: int32 [2, 196608], P(None, ('region', 'dom')), may hold values from 0 to 1535, as said below
- send_dom: int32 [2, 98304], P(None, ('region', 'dom')), may hold values from 0 to 1535, as said below
- move_dom: int32 [393216], P(('region', 'dom')), may hold values from 0 to 11, as said below
- move_slot: int32 [393216], P(('region', 'dom')), may hold values from 0 to 511, as said below
Outputs:
- new_state: float32 [3, 10, 393216], P(None, None, ('region', 'dom'))
Inputs may be any that keep to these rules, and one draw needn't show every extreme that they name: Each device holds at most 128 triangles of cluster 0, some device exactly 128, the others 128 or 32. `face_code`: codes below 1536 name a face f * 512 + e of the own device; the next 768 codes name received slots, each named by exactly one face of the device; the largest code marks a wall, named by 64 faces of each device. `send_region`: each list names faces f * 512 + e of its own device, none twice; its first 8 slots hold faces of cluster-0 triangles, the others faces of cluster-1 triangles. `send_dom`: each list names faces f * 512 + e of its own device, none twice; its first 4 slots hold faces of cluster-0 triangles, the others faces of cluster-1 triangles. `move_dom`: with move_slot, a permutation of each region's triangles; every device hands exactly 32 triangles to each other dom index of its region and keeps the rest at their own positions. `move_slot`: see move_dom; staying triangles keep their position.
All inputs are finite; a program needn't handle non-finite values.
Results may differ from a plain program's by a relative error of at most 0.0003.
Values sent between devices are 32-bit elements; how exact they have to be, the bound alone decides.
A program may use at most 32 MiB of HBM per device.

v0:
```python
import jax
import jax.numpy as jnp
from jax import lax
from jax.sharding import PartitionSpec as P

NODES = 10
POINTS = 4
MIGRANTS = 32


HIGHEST = lax.Precision.HIGHEST
FIRST_HALF = (0.5, 0.125, 1.0 / 48.0, 1.0 / 384.0)
SECOND_HALF = (0.5, 0.375, 7.0 / 48.0, 15.0 / 384.0)


def extended_2(cells, sides, width):
    for axis, dim in sides:
        count = lax.axis_size(axis)
        ends = count - 1
        head = lax.slice_in_dim(cells, 0, width, axis=dim)
        tail = lax.slice_in_dim(cells, cells.shape[dim] - width, cells.shape[dim], axis=dim)
        cells = jnp.concatenate(
            [
                lax.ppermute(tail, axis, [(i, (i + 1) % count) for i in range(ends)]),
                cells,
                lax.ppermute(head, axis, [((i + 1) % count, i) for i in range(ends)]),
            ],
            axis=dim,
        )
    return cells


def spatial(values, water_depth, metric, diff_ops):
    slopes = jnp.einsum("aij,vjn->avin", diff_ops, values, precision=HIGHEST)
    along_x = metric[0] * slopes[0] + metric[1] * slopes[1]
    along_y = metric[2] * slopes[0] + metric[3] * slopes[1]
    return -jnp.stack([along_x[1] + along_y[2], water_depth * along_x[0], water_depth * along_y[0]])


def predictor(values, water_depth, metric, diff_ops):
    series = [values]
    for degree in range(3):
        series.append(spatial(series[-1], water_depth, metric, diff_ops))
    return series


def integrate(series, factors):
    summed = factors[0] * series[0]
    for factor, member in zip(factors[1:], series[1:]):
        summed = summed + factor * member
    return summed


def face_table(values, trace_ops):
    return jnp.einsum("fqj,vjn->vqfn", trace_ops, values, precision=HIGHEST)


def normal_flux(traces, normal_x, normal_y, water_depth):
    return jnp.stack(
        [
            traces[1] * normal_x + traces[2] * normal_y,
            water_depth * traces[0] * normal_x,
            water_depth * traces[0] * normal_y,
        ]
    )


def increment(values, inside, beyond, is_wall, water_depth, metric, stiff_ops, lift_ops):
    flipped = beyond[:, ::-1]
    mirror = jnp.stack([inside[0], -inside[1], -inside[2]])
    outside = jnp.where(is_wall, mirror, flipped)
    normal_x = 2.0 * jnp.stack([-metric[1], metric[0] + metric[1], -metric[0]])
    normal_y = 2.0 * jnp.stack([-metric[3], metric[2] + metric[3], -metric[2]])
    wave_speed = jnp.sqrt(water_depth) * jnp.sqrt(normal_x * normal_x + normal_y * normal_y)
    fluxes = 0.5 * (
        normal_flux(inside, normal_x, normal_y, water_depth)
        + normal_flux(outside, normal_x, normal_y, water_depth)
    ) - 0.5 * wave_speed * (outside - inside)
    lifted = jnp.einsum("fjq,vqfn->vjn", lift_ops, fluxes, precision=HIGHEST)
    weak_slopes = jnp.einsum("aij,vjn->avin", stiff_ops, values, precision=HIGHEST)
    weak_x = metric[0] * weak_slopes[0] + metric[1] * weak_slopes[1]
    weak_y = metric[2] * weak_slopes[0] + metric[3] * weak_slopes[1]
    volume = jnp.stack([weak_x[1] + weak_y[2], water_depth * weak_x[0], water_depth * weak_y[0]])
    return volume - lifted


def swap_faces(region_part, dom_part):
    got_region = extended_2(region_part, (("region", 1),), 1)
    got_dom = extended_2(dom_part, (("dom", 1),), 1)
    return (got_region, got_dom)


def outer_traces(table, got_region, got_dom, codes_flat, elems):
    extended = jnp.concatenate(
        [
            table,
            got_region[:, 0],
            got_region[:, 3],
            got_dom[:, 0],
            got_dom[:, 3],
            jnp.zeros((table.shape[0], 1), table.dtype),
        ],
        axis=1,
    )
    return jnp.take(extended, codes_flat, axis=1).reshape(3, POINTS, 3, elems)


def shards(
    water_state,
    water_depth,
    metric,
    diff_ops,
    stiff_ops,
    trace_ops,
    lift_ops,
    cluster,
    face_code,
    send_region,
    send_dom,
    move_dom,
    move_slot,
):
    elems = water_state.shape[2]
    rows = 3 * POINTS
    reg_slots = send_region.shape[1]
    dom_slots = send_dom.shape[1]
    wall_code = 3 * elems + 2 * reg_slots + 2 * dom_slots
    codes_flat = face_code.reshape(-1)
    is_wall = face_code == wall_code
    series = predictor(water_state, water_depth, metric, diff_ops)
    early = integrate(series, FIRST_HALF)
    later = integrate(series, SECOND_HALF)
    inside_first = face_table(early, trace_ops)
    first_table = inside_first.reshape(rows, 3 * elems)
    region_part = jnp.take(first_table, send_region, axis=1)
    dom_part = jnp.take(first_table, send_dom, axis=1)
    got_region, got_dom = swap_faces(region_part, dom_part)
    beyond_first = outer_traces(first_table, got_region, got_dom, codes_flat, elems)
    midway = water_state + increment(
        early, inside_first, beyond_first, is_wall, water_depth, metric, stiff_ops, lift_ops
    )
    fine_part = integrate(predictor(midway, water_depth, metric, diff_ops), FIRST_HALF)
    second = jnp.where(cluster == 0, fine_part, later)
    inside_second = face_table(second, trace_ops)
    second_table = inside_second.reshape(rows, 3 * elems)
    region_second, dom_second = swap_faces(
        jnp.take(second_table, send_region, axis=1), jnp.take(second_table, send_dom, axis=1)
    )
    beyond_second = outer_traces(second_table, region_second, dom_second, codes_flat, elems)
    stepped = midway + increment(
        second, inside_second, beyond_second, is_wall, water_depth, metric, stiff_ops, lift_ops
    )
    peer_count = lax.axis_size("dom")
    own_dom = lax.axis_index("dom")
    leaving = move_dom != own_dom
    chosen = (move_dom[None, :] == jnp.arange(peer_count, dtype=jnp.int32)[:, None]) & leaving[
        None, :
    ]
    running = jnp.cumsum(chosen.astype(jnp.int32), axis=1)
    order_rank = jnp.sum(jnp.where(chosen, running, 0), axis=0) - 1
    buffer_slot = jnp.where(leaving, move_dom * MIGRANTS + order_rank, peer_count * MIGRANTS)
    stacked = stepped.reshape(3 * NODES, elems)
    outgoing = (
        jnp.zeros((3 * NODES, peer_count * MIGRANTS), jnp.float32)
        .at[:, buffer_slot]
        .set(stacked, mode="drop")
    )
    landing = (
        jnp.full((peer_count * MIGRANTS,), elems, jnp.int32)
        .at[buffer_slot]
        .set(move_slot, mode="drop")
    )
    arrived, places = (
        lax.all_to_all(
            outgoing.reshape(3 * NODES, peer_count, MIGRANTS),
            "dom",
            split_axis=1,
            concat_axis=1,
            tiled=True,
        ),
        lax.all_to_all(
            landing.reshape(1, peer_count, MIGRANTS), "dom", split_axis=1, concat_axis=1, tiled=True
        ),
    )
    result = stacked.at[:, places.reshape(-1)].set(
        arrived.reshape(3 * NODES, peer_count * MIGRANTS), mode="drop"
    )
    return result.reshape(3, NODES, elems)


def solution(mesh):
    placed = (
        P(None, None, ("region", "dom")),
        P(("region", "dom")),
        P(None, ("region", "dom")),
        P(),
        P(),
        P(),
        P(),
        P(("region", "dom")),
        P(None, ("region", "dom")),
        P(None, ("region", "dom")),
        P(None, ("region", "dom")),
        P(("region", "dom")),
        P(("region", "dom")),
    )
    return jax.shard_map(
        shards,
        mesh=mesh,
        in_specs=placed,
        out_specs=P(None, None, ("region", "dom")),
        check_vma=False,
    )
```

profile of v0, /device:TPU:6, one launch (start us, length us, event | category | flops | bytes accessed | tf_op | source)
XLA Modules:
  0.0 99.5 jit_solution(8706768315536375701)
XLA Ops:
  0.0 0.7 fusion.77
  0.7 0.7 compare_and_fusion.1
  1.4 0.9 slice_negate_fusion.6
  2.3 1.2 %convolution_bitcast_fusion.7 = f32[2,3,10,512]{3,2,0,1:T(8,128)S(1)} fusion(f32[3,10,512,1]{2,0,1,3:T(4,128)} %bitcast.263, f32[2,10,10]{2,0,1:T(2,128)} %param.22), kind=kOutput, calls=%fused_computation.16 | convolution fusion | flops 3686400 | bytes 185120 | tf_op jit(solution)/shard_map/aij,vjn->avin/dot_general | solution.py:34
  3.5 0.7 slice_add_fusion.7
  4.2 1.0 %convolution_bitcast_fusion.6 = f32[2,3,10,512]{3,2,1,0:T(8,128)S(1)} fusion(f32[1,10,512]{2,1,0:T(8,128)S(1)} %get-tuple-element.47, f32[1,10,512]{2,1,0:T(8,128)S(1)} %get-tuple-element.46, f32[1,10,512]{2,1,0:T(8,128)S(1)} %get-tuple-element.45, f32[2,10,10,1]{2,0,1,3:T(2,128)} %bitcast.254), kind=kOutput, calls=%fused_computation.15 | convolution fusion | flops 3732480 | bytes 185120 | tf_op jit(solution)/shard_map/aij,vjn->avin/dot_general | solution.py:34
  5.3 0.3 convolution_bitcast_fusion.5
  5.8 0.3 convolution_bitcast_fusion.11
  6.2 0.3 copy.82
  6.6 1.0 %gather_fusion = f32[512,12]{1,0:T(8,128)S(1)} fusion(f32[12,1536]{0,1:T(8,128)S(1)} %copy.82, s32[1024]{0:T(1024)S(1)} %get-tuple-element.94), kind=kCustom, calls=%fused_computation.clone | custom fusion | bytes 51200 | tf_op jit(solution)/shard_map/jit(_take)/gather | solution.py:135
  7.6 0.1 copy.83
  7.8 1.9 %collective-permute-start = (f32[12,1,256]{2,0,1:T(8,128)S(1)}, f32[12,1,256]{2,0,1:T(8,128)S(1)}, u32[]{:S(2)}, u32[]{:S(2)}) collective-permute-start(f32[12,1,256]{2,0,1:T(8,128)S(1)} %get-tuple-element.75), channel_id=1, source_target_pairs={{0,12},{12,24},{24,36},{36,48},{48,60},{60,72},{72,84},{84,96},{96... | collective-permute-start | bytes 36872 | tf_op jit(solution)/shard_map/ppermute | solution.py:24
  9.7 5.8 %collective-permute-start.1 = (f32[12,1,256]{2,0,1:T(8,128)S(1)}, f32[12,1,256]{2,0,1:T(8,128)S(1)}, u32[]{:S(2)}, u32[]{:S(2)}) collective-permute-start(f32[12,1,256]{2,0,1:T(8,128)S(1)} %get-tuple-element.74), channel_id=1, source_target_pairs={{12,0},{24,12},{36,24},{48,36},{60,48},{72,60},{84,72},{96,84},{10... | collective-permute-start | bytes 36872 | tf_op jit(solution)/shard_map/ppermute | solution.py:26
  15.5 0.7 gather_fusion.1
  16.3 4.3 %collective-permute-start.2 = (f32[12,1,128]{2,0,1:T(8,128)S(1)}, f32[12,1,128]{2,0,1:T(8,128)S(1)}, u32[]{:S(2)}, u32[]{:S(2)}) collective-permute-start(f32[12,1,128]{2,0,1:T(8,128)S(1)} %get-tuple-element.79), channel_id=1, source_target_pairs={{0,1},{1,2},{2,3},{3,4},{4,5},{5,6},{6,7},{7,8},{8,9},{9,10},{10,1... | collective-permute-start | bytes 18440 | tf_op jit(solution)/shard_map/ppermute | solution.py:24
  20.6 1.3 %collective-permute-start.3 = (f32[12,1,128]{2,0,1:T(8,128)S(1)}, f32[12,1,128]{2,0,1:T(8,128)S(1)}, u32[]{:S(2)}, u32[]{:S(2)}) collective-permute-start(f32[12,1,128]{2,0,1:T(8,128)S(1)} %get-tuple-element.78), channel_id=1, source_target_pairs={{1,0},{2,1},{3,2},{4,3},{5,4},{6,5},{7,6},{8,7},{9,8},{10,9},{11,1... | collective-permute-start | bytes 18440 | tf_op jit(solution)/shard_map/ppermute | solution.py:26
  21.9 1.2 %reduce-window.6 = s32[12,4,128]{2,0,1:T(8,128)S(1)} reduce-window(s32[12,4,128]{2,0,1:T(8,128)S(1)} %fusion.52, s32[]{:T(128)} %constant.47.clone.1), window={size=1x1x128 pad=0_0x0_0x127_0}, to_apply=%region_0.4 | reduce-window | flops 780288 | bytes 49156 | tf_op jit(solution)/shard_map/reduce-window
  23.1 0.2 slice_reduce_fusion
  23.3 0.1 select_reduce_fusion
  23.4 2.6 %scatter_custom_fusion = s32[384]{0:T(512)S(1)} fusion(s32[512]{0:T(512)S(1)} %compare_select_fusion.3, s32[512]{0:T(512)} %param.31, s32[]{:T(128)} %constant.51.clone.1), kind=kCustom, calls=%fused_computation.216 | custom fusion | bytes 2048 | tf_op jit(solution)/shard_map/scatter | solution.py:171
  26.0 0.7 reshape.445
  26.7 15.4 %all-to-all-start = ((s32[1,12,32]{2,0,1:T(1,128)}), s32[1,12,32]{2,0,1:T(1,128)S(1)}, u32[]{:S(2)}, u32[]{:S(2)}) async-start(s32[1,12,32]{2,0,1:T(1,128)} %reshape.445), calls=%async_computation | async-start | bytes 12288 | tf_op jit(solution)/shard_map/all_to_all | solution.py:181
  42.3 0.3 convolution_bitcast_fusion.4
  42.9 0.4 copy.86
  43.3 2.6 %gather_fusion.2 = f32[1536,12]{1,0:T(8,128)S(1)} fusion(f32[12,2305]{0,1:T(8,128)S(1)} %copy.86, s32[2048]{0:T(1024)S(1)} %pad_clamp_fusion), kind=kCustom, calls=%fused_computation.2.clone | custom fusion | bytes 153600 | tf_op jit(solution)/shard_map/jit(_take)/gather | solution.py:105
  45.9 0.3 select_bitcast_fusion.1
  46.2 0.3 copy.87
  46.5 0.2 rev.6
  46.8 0.3 fusion.3
  47.1 0.3 convolution_bitcast_fusion.3
  47.5 0.3 convolution_bitcast_fusion.2
  47.9 0.3 convolution_bitcast_fusion.1
  48.3 0.1 fusion.6
  48.4 0.3 convolution_bitcast_fusion.10
  48.8 0.3 copy.99
  49.0 1.0 %gather_fusion.3 = f32[512,12]{1,0:T(8,128)S(1)} fusion(f32[12,1536]{0,1:T(8,128)S(1)} %copy.99, s32[1024]{0:T(1024)S(1)} %get-tuple-element.94), kind=kCustom, calls=%fused_computation.3.clone | custom fusion | bytes 51200 | tf_op jit(solution)/shard_map/jit(_take)/gather | solution.py:147
  50.1 0.7 gather_fusion.4
  50.9 0.3 convolution_bitcast_fusion
  51.2 0.1 copy.100
  51.3 1.9 %collective-permute-start.4 = (f32[12,1,256]{2,0,1:T(8,128)S(1)}, f32[12,1,256]{2,0,1:T(8,128)S(1)}, u32[]{:S(2)}, u32[]{:S(2)}) collective-permute-start(f32[12,1,256]{2,0,1:T(8,128)S(1)} %get-tuple-element.73), channel_id=1, source_target_pairs={{0,12},{12,24},{24,36},{36,48},{48,60},{60,72},{72,84},{84,96},{96... | collective-permute-start | bytes 36872 | tf_op jit(solution)/shard_map/ppermute | solution.py:24
  53.2 5.8 %collective-permute-start.5 = (f32[12,1,256]{2,0,1:T(8,128)S(1)}, f32[12,1,256]{2,0,1:T(8,128)S(1)}, u32[]{:S(2)}, u32[]{:S(2)}) collective-permute-start(f32[12,1,256]{2,0,1:T(8,128)S(1)} %get-tuple-element.72), channel_id=1, source_target_pairs={{12,0},{24,12},{36,24},{48,36},{60,48},{72,60},{84,72},{96,84},{10... | collective-permute-start | bytes 36872 | tf_op jit(solution)/shard_map/ppermute | solution.py:26
  59.0 0.1 copy.102
  59.1 3.9 %collective-permute-start.6 = (f32[12,1,128]{2,0,1:T(8,128)S(1)}, f32[12,1,128]{2,0,1:T(8,128)S(1)}, u32[]{:S(2)}, u32[]{:S(2)}) collective-permute-start(f32[12,1,128]{2,0,1:T(8,128)S(1)} %get-tuple-element.77), channel_id=1, source_target_pairs={{0,1},{1,2},{2,3},{3,4},{4,5},{5,6},{6,7},{7,8},{8,9},{9,10},{10,1... | collective-permute-start | bytes 18440 | tf_op jit(solution)/shard_map/ppermute | solution.py:24
  63.0 1.3 %collective-permute-start.7 = (f32[12,1,128]{2,0,1:T(8,128)S(1)}, f32[12,1,128]{2,0,1:T(8,128)S(1)}, u32[]{:S(2)}, u32[]{:S(2)}) collective-permute-start(f32[12,1,128]{2,0,1:T(8,128)S(1)} %get-tuple-element.76), channel_id=1, source_target_pairs={{1,0},{2,1},{3,2},{4,3},{5,4},{6,5},{7,6},{8,7},{9,8},{10,9},{11,1... | collective-permute-start | bytes 18440 | tf_op jit(solution)/shard_map/ppermute | solution.py:26
  64.4 4.1 %collective-permute-done.7 = f32[12,1,128]{2,0,1:T(8,128)S(1)} collective-permute-done((f32[12,1,128]{2,0,1:T(8,128)S(1)}, f32[12,1,128]{2,0,1:T(8,128)S(1)}, u32[]{:S(2)}, u32[]{:S(2)}) %collective-permute-start.7) | collective-permute-done | bytes 6176 | tf_op jit(solution)/shard_map/ppermute | solution.py:26
  68.5 0.4 copy.103
  68.9 2.6 %gather_fusion.5 = f32[1536,12]{1,0:T(8,128)S(1)} fusion(f32[12,2305]{0,1:T(8,128)S(1)} %copy.103, s32[2048]{0:T(1024)S(1)} %pad_clamp_fusion), kind=kCustom, calls=%fused_computation.5.clone | custom fusion | bytes 153600 | tf_op jit(solution)/shard_map/jit(_take)/gather | solution.py:105
  71.5 0.3 select_bitcast_fusion
  71.8 0.3 copy.104
  72.2 0.2 rev.7
  72.5 0.3 fusion.1
  72.8 0.1 copy.107
  73.0 1.8 %scatter_custom_fusion.1 = f32[30,384]{0,1:T(8,128)S(1)} fusion(s32[512]{0:T(512)S(1)} %compare_select_fusion.3, f32[512,30]{1,0:T(8,128)S(1)} %copy.107, f32[]{:T(128)} %constant.14.clone.1), kind=kCustom, calls=%fused_computation.63 | custom fusion | bytes 46084 | tf_op jit(solution)/shard_map/scatter | solution.py:166
  74.7 0.9 reshape.453
  75.6 9.1 %all-to-all-start.1 = ((f32[12,1,960]{2,1,0:T(1,128)}), f32[12,1,960]{2,1,0:T(1,128)S(1)}, u32[]{:S(2)}, u32[]{:S(2)}) async-start(f32[12,1,960]{2,1,0:T(1,128)} %reshape.453), calls=%async_computation.1 | async-start | bytes 98304 | tf_op jit(solution)/shard_map/all_to_all | solution.py:174
  84.8 0.1 reshape.317
  84.9 0.1 copy.108
  85.0 10.6 %all-to-all-done.1 = f32[12,1,960]{2,1,0:T(1,128)S(1)} async-done(((f32[12,1,960]{2,1,0:T(1,128)}), f32[12,1,960]{2,1,0:T(1,128)S(1)}, u32[]{:S(2)}, u32[]{:S(2)}) %all-to-all-start.1) | async-done | bytes 46112 | tf_op jit(solution)/shard_map/all_to_all | solution.py:174
  95.6 0.5 broadcast.325
  96.1 0.8 reduce.6
  96.9 0.2 reshape.454
  97.1 1.6 %scatter_fusion = f32[30,512]{0,1:T(8,128)S(1)} fusion(f32[30,512]{0,1:T(8,128)S(1)} %copy.108, s32[384]{0:T(512)S(1)} %fusion.73, f32[384,30]{1,0:T(8,128)S(1)} %bitcast.272), kind=kCustom, calls=%fused_computation.8 | custom fusion | bytes 139776 | tf_op jit(solution)/shard_map/scatter | solution.py:185
  98.7 0.1 copy.109
  98.8 0.7 copy.110
  (102 shorter events, 1.5 us)
Async XLA Ops:
  0.0 42.3 %copy-start = (f32[2,10,10]{2,0,1:T(2,128)S(1)}, f32[2,10,10]{2,0,1:T(2,128)}, u32[]{:S(2)}) copy-start(f32[2,10,10]{2,0,1:T(2,128)} %param.23) | copy-start | bytes 2404
  0.0 5.3 %copy-start.1 = (f32[2,10,10]{2,0,1:T(2,128)S(1)}, f32[2,10,10]{2,0,1:T(2,128)}, u32[]{:S(2)}) copy-start(f32[2,10,10]{2,0,1:T(2,128)} %param.22) | copy-start | bytes 2404
  0.0 5.3 %copy-start.3 = (f32[512]{0:T(512)S(1)}, f32[512]{0:T(512)}, u32[]{:S(2)}) copy-start(f32[512]{0:T(512)} %param.20) | copy-start | bytes 6148
  3.5 2.2 %copy-start.2 = (f32[3,10,512]{2,0,1:T(4,128)S(1)}, f32[3,10,512]{2,0,1:T(4,128)}, u32[]{:S(2)}) copy-start(f32[3,10,512]{2,0,1:T(4,128)} %param.19) | copy-start | bytes 184324
  4.2 1.6 %copy-start.6 = (f32[3,4,10]{2,1,0:T(4,128)S(1)}, f32[3,4,10]{2,1,0:T(4,128)}, u32[]{:S(2)}) copy-start(f32[3,4,10]{2,1,0:T(4,128)} %param.24) | copy-start | bytes 1444
  5.7 0.9 copy-start.8
  6.1 15.7 %copy-start.4 = (s32[512]{0:T(512)S(1)}, s32[512]{0:T(512)}, u32[]{:S(2)}) copy-start(s32[512]{0:T(512)} %param.30) | copy-start | bytes 6148
  6.2 36.0 %copy-start.5 = (s32[3,512]{1,0:T(4,128)S(1)}, s32[3,512]{1,0:T(4,128)}, u32[]{:S(2)}) copy-start(s32[3,512]{1,0:T(4,128)} %param.27) | copy-start | bytes 18436
  6.5 36.1 %copy-start.7 = (s32[512]{0:T(512)S(1)}, s32[512]{0:T(512)}, u32[]{:S(2)}) copy-start(s32[512]{0:T(512)} %param.26) | copy-start | bytes 6148
  7.8 35.0 %collective-permute-start = (f32[12,1,256]{2,0,1:T(8,128)S(1)}, f32[12,1,256]{2,0,1:T(8,128)S(1)}, u32[]{:S(2)}, u32[]{:S(2)}) collective-permute-start(f32[12,1,256]{2,0,1:T(8,128)S(1)} %get-tuple-element.75), channel_id=1, source_target_pairs={{0,12},{12,24},{24,36},{36,48},{48,60},{60,72},{72,84},{84,96},{96... | collective-permute-start | bytes 36872 | tf_op jit(solution)/shard_map/ppermute | solution.py:24
  9.7 33.1 %collective-permute-start.1 = (f32[12,1,256]{2,0,1:T(8,128)S(1)}, f32[12,1,256]{2,0,1:T(8,128)S(1)}, u32[]{:S(2)}, u32[]{:S(2)}) collective-permute-start(f32[12,1,256]{2,0,1:T(8,128)S(1)} %get-tuple-element.74), channel_id=1, source_target_pairs={{12,0},{24,12},{36,24},{48,36},{60,48},{72,60},{84,72},{96,84},{10... | collective-permute-start | bytes 36872 | tf_op jit(solution)/shard_map/ppermute | solution.py:26
  16.3 26.5 %collective-permute-start.2 = (f32[12,1,128]{2,0,1:T(8,128)S(1)}, f32[12,1,128]{2,0,1:T(8,128)S(1)}, u32[]{:S(2)}, u32[]{:S(2)}) collective-permute-start(f32[12,1,128]{2,0,1:T(8,128)S(1)} %get-tuple-element.79), channel_id=1, source_target_pairs={{0,1},{1,2},{2,3},{3,4},{4,5},{5,6},{6,7},{7,8},{8,9},{9,10},{10,1... | collective-permute-start | bytes 18440 | tf_op jit(solution)/shard_map/ppermute | solution.py:24
  20.6 22.3 %collective-permute-start.3 = (f32[12,1,128]{2,0,1:T(8,128)S(1)}, f32[12,1,128]{2,0,1:T(8,128)S(1)}, u32[]{:S(2)}, u32[]{:S(2)}) collective-permute-start(f32[12,1,128]{2,0,1:T(8,128)S(1)} %get-tuple-element.78), channel_id=1, source_target_pairs={{1,0},{2,1},{3,2},{4,3},{5,4},{6,5},{7,6},{8,7},{9,8},{10,9},{11,1... | collective-permute-start | bytes 18440 | tf_op jit(solution)/shard_map/ppermute | solution.py:26
  26.7 48.9 %all-to-all-start = ((s32[1,12,32]{2,0,1:T(1,128)}), s32[1,12,32]{2,0,1:T(1,128)S(1)}, u32[]{:S(2)}, u32[]{:S(2)}) async-start(s32[1,12,32]{2,0,1:T(1,128)} %reshape.445), calls=%async_computation | async-start | bytes 12288 | tf_op jit(solution)/shard_map/all_to_all | solution.py:181
  46.1 0.7 copy-start.9
  51.3 13.1 %collective-permute-start.4 = (f32[12,1,256]{2,0,1:T(8,128)S(1)}, f32[12,1,256]{2,0,1:T(8,128)S(1)}, u32[]{:S(2)}, u32[]{:S(2)}) collective-permute-start(f32[12,1,256]{2,0,1:T(8,128)S(1)} %get-tuple-element.73), channel_id=1, source_target_pairs={{0,12},{12,24},{24,36},{36,48},{48,60},{60,72},{72,84},{84,96},{96... | collective-permute-start | bytes 36872 | tf_op jit(solution)/shard_map/ppermute | solution.py:24
  53.2 11.1 %collective-permute-start.5 = (f32[12,1,256]{2,0,1:T(8,128)S(1)}, f32[12,1,256]{2,0,1:T(8,128)S(1)}, u32[]{:S(2)}, u32[]{:S(2)}) collective-permute-start(f32[12,1,256]{2,0,1:T(8,128)S(1)} %get-tuple-element.72), channel_id=1, source_target_pairs={{12,0},{24,12},{36,24},{48,36},{60,48},{72,60},{84,72},{96,84},{10... | collective-permute-start | bytes 36872 | tf_op jit(solution)/shard_map/ppermute | solution.py:26
  59.1 5.3 %collective-permute-start.6 = (f32[12,1,128]{2,0,1:T(8,128)S(1)}, f32[12,1,128]{2,0,1:T(8,128)S(1)}, u32[]{:S(2)}, u32[]{:S(2)}) collective-permute-start(f32[12,1,128]{2,0,1:T(8,128)S(1)} %get-tuple-element.77), channel_id=1, source_target_pairs={{0,1},{1,2},{2,3},{3,4},{4,5},{5,6},{6,7},{7,8},{8,9},{9,10},{10,1... | collective-permute-start | bytes 18440 | tf_op jit(solution)/shard_map/ppermute | solution.py:24
  63.0 5.5 %collective-permute-start.7 = (f32[12,1,128]{2,0,1:T(8,128)S(1)}, f32[12,1,128]{2,0,1:T(8,128)S(1)}, u32[]{:S(2)}, u32[]{:S(2)}) collective-permute-start(f32[12,1,128]{2,0,1:T(8,128)S(1)} %get-tuple-element.76), channel_id=1, source_target_pairs={{1,0},{2,1},{3,2},{4,3},{5,4},{6,5},{7,6},{8,7},{9,8},{10,9},{11,1... | collective-permute-start | bytes 18440 | tf_op jit(solution)/shard_map/ppermute | solution.py:26
  75.6 19.9 %all-to-all-start.1 = ((f32[12,1,960]{2,1,0:T(1,128)}), f32[12,1,960]{2,1,0:T(1,128)S(1)}, u32[]{:S(2)}, u32[]{:S(2)}) async-start(f32[12,1,960]{2,1,0:T(1,128)} %reshape.453), calls=%async_computation.1 | async-start | bytes 98304 | tf_op jit(solution)/shard_map/all_to_all | solution.py:174
where the time goes:
time: 100 us; the launch traced here: 99.5 us
  starting transfers between devices  50.6 us (51%)
  local copies, waits for them, and re-layouts  21.6 us (22%)
  waiting for transfers between devices  14.7 us (15%)
  other arithmetic  6.4 us (6%)
  matrix products  5.19 us (5%)
    all_to_all x1, starting transfers between devices, shards(): lax.all_to_all(landing.reshape(1, peer_count, MIGRANTS), 'dom', split_axi...  15.4 us
    ppermute x4, starting transfers between devices, extended_2(): lax.ppermute(head, axis, [((i + 1) % count, i) for i in range(ends)])  14.1 us
    ppermute x4, starting transfers between devices, extended_2(): lax.ppermute(tail, axis, [(i, (i + 1) % count) for i in range(ends)])  12 us
    all_to_all x1, waiting for transfers between devices, shards(): lax.all_to_all(outgoing.reshape(3 * NODES, peer_count, MIGRANTS), 'dom',...  10.6 us
    all_to_all x1, starting transfers between devices, shards(): lax.all_to_all(outgoing.reshape(3 * NODES, peer_count, MIGRANTS), 'dom',...  9.1 us
    gather x2, local copies, waits for them, and re-layouts, outer_traces(): return jnp.take(extended, codes_flat, axis=1).reshape(3, POINTS, 3, elems)  5.19 us
    ppermute x4, waiting for transfers between devices, extended_2(): lax.ppermute(head, axis, [((i + 1) % count, i) for i in range(ends)])  4.11 us
    dot_general x6, matrix products, spatial(): slopes = jnp.einsum('aij,vjn->avin', diff_ops, values, precision=HIGHEST)  3.44 us
  transfers between devices with their start and end apart: 10, of which 2 were waited for; matrix products, arithmetic and copies ran while one was open for 22% of the time, Pallas kernels for 0%

commit v1 on v0

v1 whole, which is shorter than its diff:
```python
import jax
import jax.numpy as jnp
from jax import lax
from jax.experimental import pallas as pl
from jax.experimental.pallas import tpu as pltpu
from jax.sharding import PartitionSpec as P

MESH = pl.DeviceIdType.MESH
HIGHEST = lax.Precision.HIGHEST
F32 = jnp.float32
BF16 = jnp.bfloat16
NODES = 10
FIRST_HALF = (0.5, 0.125, 1.0 / 48.0, 1.0 / 384.0)
SECOND_HALF = (0.5, 0.375, 7.0 / 48.0, 15.0 / 384.0)
MIGRANTS = 32
REG_FINE = 8
DOM_FINE = 4


def iota(shape, dim):
    return lax.broadcasted_iota(jnp.int32, shape, dim)


def ones_where(mask):
    return jnp.where(mask, 1.0, 0.0).astype(F32)


def dot(a, b):
    return jnp.dot(a, b, preferred_element_type=F32)


def exact(a, b):
    return jnp.dot(a, b, preferred_element_type=F32, precision=HIGHEST)


def dot_nt(a, b, precision=None):
    return lax.dot_general(
        a, b, (((1,), (1,)), ((), ())), preferred_element_type=F32, precision=precision
    )


def split_state(values):
    hi = values.astype(BF16)
    lo = (values - hi.astype(F32)).astype(BF16)
    return jnp.concatenate([hi, lo, hi], axis=0)


def split_matrix(wide, low_from):
    hi = wide.astype(BF16).astype(F32)
    lo = wide - hi
    return jnp.where(iota(wide.shape, 1) >= low_from, lo, hi).astype(BF16)


def var_of(row):
    return (row >= NODES).astype(jnp.int32) + (row >= 2 * NODES).astype(jnp.int32)


def state_columns(count):
    column = iota((NODES, count), 1) & 31
    node = column - NODES * var_of(column)
    return ones_where((node == iota((NODES, count), 0)) & (column < 3 * NODES))


def slope_matrix(ops_ref, sign):
    rows, cols = 96, 96
    row = iota((rows, NODES), 0)
    local = jnp.where(row < 64, row & 31, row & 15)
    node = local - NODES * var_of(local)
    second = ((row >= 32) & (row < 64)) | (row >= 80)
    valid = local < jnp.where(row < 64, 3 * NODES, NODES)
    hit = (node == iota((rows, NODES), 1)) & valid
    picked = exact(ones_where(hit & ~second), ops_ref[:, 0, :]) + exact(
        ones_where(hit & second), ops_ref[:, 1, :]
    )
    wide = exact(picked, state_columns(cols)) * sign
    row = iota((rows, cols), 0)
    local = row & 31
    source = jnp.where(row < 64, (local < NODES).astype(jnp.int32), 2)
    column = iota((rows, cols), 1) & 31
    wide = jnp.where(source == var_of(column), wide, 0.0)
    return split_matrix(wide, 64)


def trace_matrix(trace_ref):
    rows, cols = 96, 96
    row = iota((rows, 4), 0)
    point = row & 3
    point = jnp.where(row < 48, 3 - point, point)
    face = (row >> 4) - jnp.where(row < 48, 0, 3)
    picked = jnp.zeros((rows, NODES), F32)
    for f in range(3):
        pick = ones_where((point == iota((rows, 4), 1)) & (face == f))
        picked = picked + exact(pick, trace_ref[f])
    wide = exact(picked, state_columns(cols))
    part = (iota((rows, cols), 0) >> 2) & 3
    source = jnp.where(part == 3, 0, part)
    column = iota((rows, cols), 1) & 31
    wide = jnp.where(source == var_of(column), wide, 0.0)
    return split_matrix(wide, 64)


def lift_matrix(lift_ref):
    rows, cols = 32, 288
    row = iota((rows, NODES), 0)
    node = row - NODES * var_of(row)
    pick = ones_where((node == iota((rows, NODES), 1)) & (row < 3 * NODES))
    wide = jnp.zeros((rows, cols), F32)
    column = iota((4, cols), 1)
    third = column - 96 * ((column >= 96).astype(jnp.int32) + (column >= 192).astype(jnp.int32))
    for f in range(3):
        points = dot_nt(pick, lift_ref[f], HIGHEST)
        place = ones_where(((third >> 5) == f) & ((third & 3) == iota((4, cols), 0)))
        wide = wide + exact(points, place)
    column = iota((rows, cols), 1)
    third = column - 96 * ((column >= 96).astype(jnp.int32) + (column >= 192).astype(jnp.int32))
    jump = (third & 16) != 0
    part = (third >> 2) & 3
    var = var_of(iota((rows, cols), 0))
    centre = (
        ((var == 0) & ((part == 1) | (part == 2)))
        | ((var == 1) & (part == 0))
        | ((var == 2) & (part == 3))
    )
    factor = jnp.where(jump, ones_where(part == var), -ones_where(centre))
    return split_matrix(wide * factor, 192)


def combine(slopes, alpha):
    a1, a2, a3, a4 = alpha
    both = a1 * slopes[0:32] + a2 * slopes[32:64]
    top = a3 * slopes[64:80] + a4 * slopes[80:96]
    return jnp.concatenate([both[0:16] + top, both[16:32]], axis=0)


def pick_columns(load, sources, block, lane, start):
    out = start
    for k in sources:
        found = jnp.take_along_axis(load(k), lane, axis=1)
        out = jnp.where(block == k, found, out)
    return out


def step_kernel(
    n_region,
    n_dom,
    elems,
    state_ref,
    depth_ref,
    metric_ref,
    diff_ref,
    stiff_ref,
    trace_ref,
    lift_ref,
    cluster_ref,
    code_ref,
    send_reg_ref,
    send_dom_ref,
    move_dom_ref,
    move_slot_ref,
    out_ref,
    dense,
    tab_a,
    tab_b,
    tab_c,
    beyond,
    out_reg,
    out_dom,
    in_reg,
    in_dom,
    out_fine,
    in_fine,
    land_out,
    land_in,
    tile_out,
    tile_in,
    ss_reg,
    rs_reg,
    ss_dom,
    rs_dom,
    ss_fine,
    rs_fine,
    ss_land,
    rs_land,
    ss_tile,
    rs_tile,
):
    r = lax.axis_index("region")
    d = lax.axis_index("dom")
    blocks = elems // 128
    has_low = r > 0
    has_high = r < n_region - 1
    dom_low = d > 0
    dom_high = d < n_dom - 1
    sides = (
        (has_high, {"region": r + 1}, 1, 0),
        (has_low, {"region": r - 1}, 0, 1),
        (dom_high, {"dom": d + 1}, 1, 0),
        (dom_low, {"dom": d - 1}, 0, 1),
    )
    comes = (has_low, has_high, dom_low, dom_high)

    barrier = pltpu.get_barrier_semaphore()
    for exists, device, _, _ in sides[:2]:

        @pl.when(exists)
        def _():
            pl.semaphore_signal(barrier, inc=1, device_id=device, device_id_type=MESH)

    for k in range(1, n_dom):
        pl.semaphore_signal(
            barrier, inc=1, device_id={"dom": lax.rem(d + k, n_dom)}, device_id_type=MESH
        )

    dense[30:32, :] = jnp.zeros((2, elems), F32)
    for v in range(3):
        dense[NODES * v : NODES * (v + 1), :] = state_ref[:, v, :]
    state = dense[...]
    depth = depth_ref[...]
    m0, m1, m2, m3 = (metric_ref[i : i + 1, :] for i in range(4))

    row = iota((32, elems), 0)
    a1 = jnp.where(row < 10, m0, jnp.where(row < 20, depth * m0, depth * m2))
    a2 = jnp.where(row < 10, m1, jnp.where(row < 20, depth * m1, depth * m3))
    top = row[0:16] < 10
    a3 = jnp.where(top, m2, 0.0)
    a4 = jnp.where(top, m3, 0.0)
    alpha = (a1, a2, a3, a4)

    slope = slope_matrix(diff_ref, -1.0)
    traces = trace_matrix(trace_ref)

    def series_of(values):
        series = [values]
        for _ in range(3):
            series.append(combine(dot(slope, split_state(series[-1])), alpha))
        return series

    def integrate(series, factors):
        summed = factors[0] * series[0]
        for factor, member in zip(factors[1:], series[1:]):
            summed = summed + factor * member
        return summed

    series = series_of(state)
    early = integrate(series, FIRST_HALF)
    later = integrate(series, SECOND_HALF)
    early_split = split_state(early)
    tab_a[...] = dot(traces, early_split)
    tab_b[...] = dot(traces[0:48], split_state(later))

    def source(table):
        def load(k):
            f, b = divmod(k, blocks)
            return table[16 * f : 16 * f + 16, 128 * b : 128 * b + 128]

        return load

    def spread(vector):
        return jnp.broadcast_to(vector, (16, 128))

    own = range(3 * blocks)
    for which, table in enumerate((tab_a, tab_b)):
        for lane_row in range(2):
            for b in range(2):
                index = spread(send_reg_ref[lane_row : lane_row + 1, 128 * b : 128 * b + 128])
                out_reg[which, lane_row, b] = pick_columns(
                    source(table), own, index >> 7, index & 127, jnp.zeros((16, 128), F32)
                )
            index = spread(send_dom_ref[lane_row : lane_row + 1, :])
            out_dom[which, lane_row] = pick_columns(
                source(table), own, index >> 7, index & 127, jnp.zeros((16, 128), F32)
            )

    lanes = iota((1, elems), 1)
    offset = move_dom_ref[...] - d
    offset = jnp.where(offset < 0, offset + n_dom, offset)
    chosen = jnp.where(iota((16, elems), 0) == offset, 1.0, 0.0)
    before = jnp.where(iota((elems, elems), 0) < iota((elems, elems), 1), 1.0, 0.0).astype(BF16)
    rank = jnp.sum(chosen * dot(chosen.astype(BF16), before), axis=0, keepdims=True)
    slots = n_dom * MIGRANTS
    padded = 384 if slots <= 384 else 128 * (-(-slots // 128))
    position = jnp.where(offset == 0, -1, offset * MIGRANTS + rank.astype(jnp.int32))
    inverse = jnp.where(iota((padded, elems), 0) == position, 1.0, 0.0).astype(BF16)
    place = move_slot_ref[...]
    which_row = iota((8, elems), 0)
    facts = jnp.where(
        which_row == 0,
        lanes >> 1,
        jnp.where(
            which_row == 1, lanes & 1, jnp.where(which_row == 2, place >> 1, place & 1)
        ),
    )
    facts = jnp.where(which_row < 4, facts, 0).astype(F32).astype(BF16)
    found = dot_nt(facts, inverse).astype(jnp.int32)
    leaves = found[0:1] * 2 + found[1:2]
    lands = found[2:3] * 2 + found[3:4]
    for k in range(1, n_dom):
        land_out[k] = lands[:, 128 * (k // 4) : 128 * (k // 4) + 128]

    for i in range(2):

        @pl.when(jnp.logical_not(comes[i]))
        def _():
            in_reg[:, i] = jnp.zeros(in_reg.shape[0:1] + in_reg.shape[2:], F32)

        @pl.when(jnp.logical_not(comes[2 + i]))
        def _():
            in_dom[:, i] = jnp.zeros(in_dom.shape[0:1] + in_dom.shape[2:], F32)

    for i in range(4):

        @pl.when(jnp.logical_not(comes[i]))
        def _():
            in_fine[i] = jnp.zeros((16, 128), F32)

    pl.semaphore_wait(
        barrier, (n_dom - 1) + has_low.astype(jnp.int32) + has_high.astype(jnp.int32)
    )

    def copies_a(which):
        copies = []
        for i, (exists, device, lane_row, at) in enumerate(sides):
            regional = i < 2
            copies.append(
                (
                    exists,
                    comes[2 * (i // 2) + at],
                    pltpu.make_async_remote_copy(
                        src_ref=(out_reg if regional else out_dom).at[which, lane_row],
                        dst_ref=(in_reg if regional else in_dom).at[which, at],
                        send_sem=(ss_reg if regional else ss_dom).at[which, at],
                        recv_sem=(rs_reg if regional else rs_dom).at[which, at],
                        device_id=device,
                        device_id_type=MESH,
                    ),
                )
            )
        return copies

    def start(copies):
        for exists, _, copy in copies:
            pl.when(exists)(copy.start)

    def wait_recv(copies):
        for _, arrives, copy in copies:
            pl.when(arrives)(copy.wait_recv)

    def wait_send(copies):
        for exists, _, copy in copies:
            pl.when(exists)(copy.wait_send)

    first_copies = copies_a(0)
    late_copies = copies_a(1)
    start(first_copies)
    start(late_copies)

    def peer_copies(src, dst, ss, rs):
        return {
            k: pltpu.make_async_remote_copy(
                src_ref=src.at[k],
                dst_ref=dst.at[k],
                send_sem=ss.at[k],
                recv_sem=rs.at[k],
                device_id={"dom": lax.rem(d + k, n_dom)},
                device_id_type=MESH,
            )
            for k in range(1, n_dom)
        }

    nearest = sorted(range(1, n_dom), key=lambda k: min(k, n_dom - k))
    land_copies = peer_copies(land_out, land_in, ss_land, rs_land)
    for k in nearest[::-1]:
        land_copies[k].start()

    stiff = slope_matrix(stiff_ref, 1.0)
    lift = lift_matrix(lift_ref)
    half_x = (-m1, m0 + m1, -m0)
    half_y = (-m3, m2 + m3, -m2)
    root = jnp.sqrt(depth)
    rows16 = iota((16, elems), 0)
    centre_by, jump_by = [], []
    for f in range(3):
        hx, hy = half_x[f], half_y[f]
        centre_by.append(
            jnp.where(
                rows16 < 4,
                depth * hx,
                jnp.where(rows16 < 8, hx, jnp.where(rows16 < 12, hy, depth * hy)),
            )
        )
        jump_by.append(root * jnp.sqrt(hx * hx + hy * hy))
    mirror = jnp.where((iota((16, 128), 0) >= 4) & (iota((16, 128), 0) < 12), -1.0, 1.0)
    first_code = 3 * elems
    regional = 2 * send_reg_ref.shape[1]

    def code_of(f, b):
        return spread(code_ref[f : f + 1, 128 * b : 128 * b + 128])

    def local_part(table):
        for f in range(3):
            for b in range(blocks):
                code = code_of(f, b)
                wall = mirror * table[48 + 16 * f : 64 + 16 * f, 128 * b : 128 * b + 128]
                beyond[f, b] = pick_columns(source(table), own, code >> 7, code & 127, wall)

    def remote_part(which, fine):
        def load(k):
            k = k - 3 * blocks
            if k < 4:
                return in_reg[which, k // 2, k % 2]
            return in_dom[which, k - 4]

        for f in range(3):
            for b in range(blocks):
                code = code_of(f, b)
                beyond[f, b] = pick_columns(
                    load,
                    range(3 * blocks, 3 * blocks + 6),
                    code >> 7,
                    code & 127,
                    beyond[f, b],
                )

    def fine_column(code):
        slot = code - first_code
        reg = slot & 255
        from_reg = jnp.where(
            (slot >= 0) & (slot < regional) & (reg < REG_FINE), (slot >> 8) * REG_FINE + reg, -1
        )
        past = slot - regional
        dom = past & 127
        return jnp.where(
            (past >= 0) & (past < 256) & (dom < DOM_FINE),
            2 * REG_FINE + (past >> 7) * DOM_FINE + dom,
            from_reg,
        )

    def increment(values_split, table):
        volume = combine(dot(stiff, values_split), alpha)
        parts = []
        for f in range(3):
            outside = jnp.concatenate([beyond[f, b] for b in range(blocks)], axis=1)
            inside = table[48 + 16 * f : 64 + 16 * f, :]
            parts.append(centre_by[f] * (outside + inside))
            parts.append(jump_by[f] * (outside - inside))
        return volume + dot(lift, split_state(jnp.concatenate(parts, axis=0)))

    local_part(tab_a)
    wait_recv(first_copies)
    remote_part(0, False)
    midway = state + increment(early_split, tab_a)
    fine = integrate(series_of(midway), FIRST_HALF)
    second = jnp.where(cluster_ref[...] == 0, fine, later)
    second_split = split_state(second)
    tab_c[...] = dot(traces, second_split)

    lane = iota((1, 128), 1)
    wanted = jnp.where(
        lane < REG_FINE,
        send_reg_ref[1:2, 0:128],
        jnp.where(
            lane < 2 * REG_FINE,
            pltpu.roll(send_reg_ref[0:1, 0:128], REG_FINE, 1),
            jnp.where(
                lane < 2 * REG_FINE + DOM_FINE,
                pltpu.roll(send_dom_ref[1:2, :], 2 * REG_FINE, 1),
                pltpu.roll(send_dom_ref[0:1, :], 2 * REG_FINE + DOM_FINE, 1),
            ),
        ),
    )
    wanted = spread(wanted)
    out_fine[...] = pick_columns(
        source(tab_c), own, wanted >> 7, wanted & 127, jnp.zeros((16, 128), F32)
    )
    fine_copies = []
    for i, (exists, device, _, at) in enumerate(sides):
        fine_copies.append(
            (
                exists,
                comes[2 * (i // 2) + at],
                pltpu.make_async_remote_copy(
                    src_ref=out_fine,
                    dst_ref=in_fine.at[i],
                    send_sem=ss_fine.at[i],
                    recv_sem=rs_fine.at[i],
                    device_id=device,
                    device_id_type=MESH,
                ),
            )
        )
    start(fine_copies)

    local_part(tab_c)
    wait_recv(late_copies)
    remote_part(1, True)
    for k in range(1, n_dom):
        land_copies[k].wait_recv()
    kk = iota((1, 128), 1)
    stack = []
    for q in range(padded // 128):
        row_q = jnp.full((1, 128), -1, jnp.int32)
        for k in range(4 * q, min(4 * q + 4, n_dom)):
            if k > 0:
                row_q = jnp.where((kk >> 5) == (k & 3), land_in[k], row_q)
        stack.append(row_q)
    places = jnp.concatenate(stack, axis=1)
    comes_here = jnp.where(iota((elems, padded), 0) == places, 1.0, 0.0).astype(BF16)
    column = iota((8, padded), 1)
    row8 = iota((8, padded), 0)
    facts = jnp.where(row8 == 0, column >> 1, jnp.where(row8 == 1, column & 1, 1))
    found = dot_nt(facts.astype(F32).astype(BF16), comes_here).astype(jnp.int32)
    origin = jnp.where(found[2:3] > 0, found[0:1] * 2 + found[1:2], -1)

    wait_recv(fine_copies)
    lane16 = iota((16, 128), 1)
    fresh = jnp.where(
        lane16 < REG_FINE,
        in_fine[0],
        jnp.where(
            lane16 < 2 * REG_FINE,
            in_fine[1],
            jnp.where(lane16 < 2 * REG_FINE + DOM_FINE, in_fine[2], in_fine[3]),
        ),
    )
    for f in range(3):
        for b in range(blocks):
            column = fine_column(code_of(f, b))
            found = jnp.take_along_axis(fresh, column & 127, axis=1)
            beyond[f, b] = jnp.where(column >= 0, found, beyond[f, b])
    dense[...] = midway + increment(second_split, tab_c)

    def cell(g, b):
        return dense[8 * g : 8 * g + 8, 128 * b : 128 * b + 128]

    group = iota((8, 128), 1) >> 5
    tile_copies = peer_copies(tile_out, tile_in, ss_tile, rs_tile)
    packed = {}
    for q in range(padded // 128):
        index = jnp.broadcast_to(leaves[:, 128 * q : 128 * q + 128], (8, 128))
        for g in range(4):
            packed[g, q] = pick_columns(
                lambda b: cell(g, b), range(blocks), index >> 7, index & 127, jnp.zeros((8, 128), F32)
            )
    for k in nearest[::-1]:
        tile = jnp.zeros((8, 128), F32)
        for g in range(4):
            shift = (32 * (g - (k & 3))) % 128
            moved = packed[g, k // 4]
            if shift:
                moved = pltpu.roll(moved, shift, 1)
            tile = jnp.where(group == g, moved, tile)
        tile_out[k] = tile
        tile_copies[k].start()

    result = {(g, b): cell(g, b) for g in range(4) for b in range(blocks)}
    for k in nearest:
        tile_copies[k].wait_recv()
        tile = tile_in[k]
        for b in range(blocks):
            index = jnp.broadcast_to(origin[:, 128 * b : 128 * b + 128], (8, 128))
            here = (index >> 5) == k
            for g in range(4):
                found = jnp.take_along_axis(tile, (index & 31) + 32 * g, axis=1)
                result[g, b] = jnp.where(here, found, result[g, b])
    for g in range(4):
        for b in range(blocks):
            dense[8 * g : 8 * g + 8, 128 * b : 128 * b + 128] = result[g, b]
    for v in range(3):
        out_ref[:, v, :] = dense[NODES * v : NODES * (v + 1), :]

    wait_send(first_copies)
    wait_send(late_copies)
    wait_send(fine_copies)
    for k in range(1, n_dom):
        land_copies[k].wait_send()
        tile_copies[k].wait_send()


def shards(n_region, n_dom, *args):
    (
        water_state,
        water_depth,
        metric,
        diff_ops,
        stiff_ops,
        trace_ops,
        lift_ops,
        cluster,
        face_code,
        send_region,
        send_dom,
        move_dom,
        move_slot,
    ) = args
    elems = water_state.shape[2]
    blocks = elems // 128
    vmem = pl.BlockSpec(memory_space=pltpu.VMEM)
    dma = pltpu.SemaphoreType.DMA

    def kernel(*refs):
        step_kernel(n_region, n_dom, elems, *refs)

    result = pl.pallas_call(
        kernel,
        out_shape=jax.ShapeDtypeStruct((NODES, 3, elems), F32),
        in_specs=[vmem] * 13,
        out_specs=vmem,
        scratch_shapes=[
            pltpu.VMEM((32, elems), F32),
            pltpu.VMEM((96, elems), F32),
            pltpu.VMEM((48, elems), F32),
            pltpu.VMEM((96, elems), F32),
            pltpu.VMEM((3, blocks, 16, 128), F32),
            pltpu.VMEM((2, 2, 2, 16, 128), F32),
            pltpu.VMEM((2, 2, 16, 128), F32),
            pltpu.VMEM((2, 2, 2, 16, 128), F32),
            pltpu.VMEM((2, 2, 16, 128), F32),
            pltpu.VMEM((16, 128), F32),
            pltpu.VMEM((4, 16, 128), F32),
            pltpu.VMEM((n_dom, 1, 128), jnp.int32),
            pltpu.VMEM((n_dom, 1, 128), jnp.int32),
            pltpu.VMEM((n_dom, 8, 128), F32),
            pltpu.VMEM((n_dom, 8, 128), F32),
            dma((2, 2)),
            dma((2, 2)),
            dma((2, 2)),
            dma((2, 2)),
            dma((4,)),
            dma((4,)),
            dma((n_dom,)),
            dma((n_dom,)),
            dma((n_dom,)),
            dma((n_dom,)),
        ],
        compiler_params=pltpu.CompilerParams(collective_id=0, has_side_effects=True),
        name="wave_step",
    )(
        jnp.transpose(water_state, (1, 0, 2)),
        water_depth.reshape(1, elems),
        metric,
        jnp.transpose(diff_ops, (1, 0, 2)),
        jnp.transpose(stiff_ops, (1, 0, 2)),
        trace_ops,
        jnp.transpose(lift_ops, (0, 2, 1)),
        cluster.reshape(1, elems),
        face_code,
        send_region,
        send_dom,
        move_dom.reshape(1, elems),
        move_slot.reshape(1, elems),
    )
    return jnp.transpose(result, (1, 0, 2))


def solution(mesh):
    both = ("region", "dom")
    wide, flat = P(None, both), P(both)
    placed = (
        P(None, None, both),
        flat,
        wide,
        P(),
        P(),
        P(),
        P(),
        flat,
        wide,
        wide,
        wide,
        flat,
        flat,
    )
    n_region, n_dom = mesh.shape["region"], mesh.shape["dom"]

    def step(*args):
        return shards(n_region, n_dom, *args)

    return jax.shard_map(
        step,
        mesh=mesh,
        in_specs=placed,
        out_specs=P(None, None, both),
        check_vma=False,
    )
```

time: 100 us -> 34.5 us (0.34)
  starting transfers between devices: 50.6 us -> 0 us
  Pallas kernels: 0 us -> 32.8 us
  local copies, waits for them, and re-layouts: 21.6 us -> 1.54 us
  waiting for transfers between devices: 14.7 us -> 0 us
  other arithmetic: 6.4 us -> 0 us
  matrix products: 5.19 us -> 0 us
    pallas_call x0 -> x1, Pallas kernels: none -> 32.8 us  [shards(): pl.pallas_call(kernel, out_shape=jax.ShapeDtypeStruct((NODES, 3, elems),...]
    ppermute x8 -> x0, starting transfers between devices: 26.1 us -> none  [the longest x4 14.1 us: extended_2(): lax.ppermute(head, axis, [((i + 1) % count, i) for i in range(ends)])]
    all_to_all x2 -> x0, starting transfers between devices: 24.5 us -> none  [the longest x1 15.4 us: shards(): lax.all_to_all(landing.reshape(1, peer_count, MIGRANTS), 'dom', split_axi...]
    all_to_all x2 -> x0, waiting for transfers between devices: 10.6 us -> none  [the longest x1 10.6 us: shards(): lax.all_to_all(outgoing.reshape(3 * NODES, peer_count, MIGRANTS), 'dom',...]
    gather x10 -> x0, local copies, waits for them, and re-layouts: 9.09 us -> none  [the longest x2 5.19 us: outer_traces(): return jnp.take(extended, codes_flat, axis=1).reshape(3, POINTS, 3, elems)]
    scatter x4 -> x0, local copies, waits for them, and re-layouts: 6.03 us -> none  [the longest x1 2.59 us: shards(): landing = jnp.full((peer_count * MIGRANTS,), elems, jnp.int32).at[buffer_...]
    dot_general x12 -> x0, matrix products: 5.19 us -> none  [the longest x6 3.44 us: spatial(): slopes = jnp.einsum('aij,vjn->avin', diff_ops, values, precision=HIGHEST)]
    ppermute x8 -> x0, waiting for transfers between devices: 4.12 us -> none  [the longest x4 4.11 us: extended_2(): lax.ppermute(head, axis, [((i + 1) % count, i) for i in range(ends)])]
  transfers between devices with their start and end apart: 10 -> 0, of which waited for: 2 -> 0; matrix products, arithmetic and copies ran while one was open for 22% -> 0% of each run, Pallas kernels for 0% -> 0%
where the time goes in v1:
time: 34.5 us; the launch traced here: 34.3 us
  Pallas kernels  32.8 us (95%)
  local copies, waits for them, and re-layouts  1.54 us (4%)
    pallas_call x1, Pallas kernels, shards(): pl.pallas_call(kernel, out_shape=jax.ShapeDtypeStruct((NODES, 3, elems),...  32.8 us
    unnamed x1, local copies, waits for them, and re-layouts  1.54 us

profile of v1, /device:TPU:6, one launch (start us, length us, event | category | flops | bytes accessed | tf_op | source)
XLA Modules:
  0.0 34.3 jit_solution(13595610059042627621)
XLA Ops:
  0.0 32.8 %wave_step.1 = f32[10,3,512]{2,1,0:T(4,128)} custom-call(f32[10,3,512]{2,1,0:T(4,128)} %bitcast.10, f32[1,512]{1,0:T(1,128)} %bitcast.14, f32[4,512]{1,0:T(4,128)} %refs_2_.1, f32[10,2,10]{2,1,0:T(2,128)} %bitcast.11, f32[10,2,10]{2,1,0:T(2,128)} %bitcast.12, f32[3,4,10]{2,1,0:T(4,128)} %refs_5_.1, f32[3,4,10]{2,1,0:T(4,128)} %bitcast.13, ...), custom_call_target="tpu_custom_call" | custom-call | tf_op jit(solution)/shard_map/wave_step/pallas_call | solution.py:603
  32.8 1.5 %copy.15 = f32[3,10,512]{2,0,1:T(4,128)} copy(f32[3,10,512]{2,0,1:T(4,128)} %bitcast.9) | data formatting | bytes 122880

commit v2 on v1

--- a/solution.py
+++ b/solution.py
@@ -158,6 +158,37 @@
     move_dom_ref,
     move_slot_ref,
     out_ref,
+    *scratch,
+):
+    hbm_refs = (
+        state_ref,
+        depth_ref,
+        metric_ref,
+        diff_ref,
+        stiff_ref,
+        trace_ref,
+        lift_ref,
+        cluster_ref,
+        code_ref,
+        send_reg_ref,
+        send_dom_ref,
+        move_dom_ref,
+        move_slot_ref,
+    )
+    step_body(
+        n_region, n_dom, elems, hbm_refs, out_ref, scratch[: len(hbm_refs)], *scratch[len(hbm_refs) :]
+    )
+
+
+def step_body(
+    n_region,
+    n_dom,
+    elems,
+    hbm_refs,
+    out_ref,
+    local_refs,
+    in_sem,
+    ready,
     dense,
     tab_a,
     tab_b,
@@ -199,17 +230,51 @@
     )
     comes = (has_low, has_high, dom_low, dom_high)
 
+    loads = [
+        pltpu.make_async_copy(src, dst, in_sem.at[i])
+        for i, (src, dst) in enumerate(zip(hbm_refs, local_refs))
+    ]
     barrier = pltpu.get_barrier_semaphore()
+
+    def ring(k):
+        return {"dom": lax.rem(d + k + n_dom, n_dom)}
+
+    for i in (0, 1, 2, 3, 5, 9, 10):
+        loads[i].start()
     for exists, device, _, _ in sides[:2]:
 
         @pl.when(exists)
         def _():
             pl.semaphore_signal(barrier, inc=1, device_id=device, device_id_type=MESH)
 
-    for k in range(1, n_dom):
-        pl.semaphore_signal(
-            barrier, inc=1, device_id={"dom": lax.rem(d + k, n_dom)}, device_id_type=MESH
-        )
+    for k in (1, -1):
+        pl.semaphore_signal(barrier, inc=1, device_id=ring(k), device_id_type=MESH)
+    for i in (4, 6, 7, 8, 11, 12):
+        loads[i].start()
+
+    def announce(stage, reach):
+        for k in (reach, -reach):
+            pl.semaphore_signal(
+                ready.at[stage], inc=1, device_id=ring(k), device_id_type=MESH
+            )
+
+    (
+        state_ref,
+        depth_ref,
+        metric_ref,
+        diff_ref,
+        stiff_ref,
+        trace_ref,
+        lift_ref,
+        cluster_ref,
+        code_ref,
+        send_reg_ref,
+        send_dom_ref,
+        move_dom_ref,
+        move_slot_ref,
+    ) = local_refs
+    for i in (0, 1, 2, 3, 5, 9, 10):
+        loads[i].wait()
 
     dense[30:32, :] = jnp.zeros((2, elems), F32)
     for v in range(3):
@@ -243,10 +308,8 @@
 
     series = series_of(state)
     early = integrate(series, FIRST_HALF)
-    later = integrate(series, SECOND_HALF)
     early_split = split_state(early)
-    tab_a[...] = dot(traces, early_split)
-    tab_b[...] = dot(traces[0:48], split_state(later))
+    tab_a[0:48] = dot(traces[0:48], early_split)
 
     def source(table):
         def load(k):
@@ -259,7 +322,8 @@
         return jnp.broadcast_to(vector, (16, 128))
 
     own = range(3 * blocks)
-    for which, table in enumerate((tab_a, tab_b)):
+
+    def gather_sends(which, table):
         for lane_row in range(2):
             for b in range(2):
                 index = spread(send_reg_ref[lane_row : lane_row + 1, 128 * b : 128 * b + 128])
@@ -271,51 +335,7 @@
                 source(table), own, index >> 7, index & 127, jnp.zeros((16, 128), F32)
             )
 
-    lanes = iota((1, elems), 1)
-    offset = move_dom_ref[...] - d
-    offset = jnp.where(offset < 0, offset + n_dom, offset)
-    chosen = jnp.where(iota((16, elems), 0) == offset, 1.0, 0.0)
-    before = jnp.where(iota((elems, elems), 0) < iota((elems, elems), 1), 1.0, 0.0).astype(BF16)
-    rank = jnp.sum(chosen * dot(chosen.astype(BF16), before), axis=0, keepdims=True)
-    slots = n_dom * MIGRANTS
-    padded = 384 if slots <= 384 else 128 * (-(-slots // 128))
-    position = jnp.where(offset == 0, -1, offset * MIGRANTS + rank.astype(jnp.int32))
-    inverse = jnp.where(iota((padded, elems), 0) == position, 1.0, 0.0).astype(BF16)
-    place = move_slot_ref[...]
-    which_row = iota((8, elems), 0)
-    facts = jnp.where(
-        which_row == 0,
-        lanes >> 1,
-        jnp.where(
-            which_row == 1, lanes & 1, jnp.where(which_row == 2, place >> 1, place & 1)
-        ),
-    )
-    facts = jnp.where(which_row < 4, facts, 0).astype(F32).astype(BF16)
-    found = dot_nt(facts, inverse).astype(jnp.int32)
-    leaves = found[0:1] * 2 + found[1:2]
-    lands = found[2:3] * 2 + found[3:4]
-    for k in range(1, n_dom):
-        land_out[k] = lands[:, 128 * (k // 4) : 128 * (k // 4) + 128]
-
-    for i in range(2):
-
-        @pl.when(jnp.logical_not(comes[i]))
-        def _():
-            in_reg[:, i] = jnp.zeros(in_reg.shape[0:1] + in_reg.shape[2:], F32)
-
-        @pl.when(jnp.logical_not(comes[2 + i]))
-        def _():
-            in_dom[:, i] = jnp.zeros(in_dom.shape[0:1] + in_dom.shape[2:], F32)
-
-    for i in range(4):
-
-        @pl.when(jnp.logical_not(comes[i]))
-        def _():
-            in_fine[i] = jnp.zeros((16, 128), F32)
-
-    pl.semaphore_wait(
-        barrier, (n_dom - 1) + has_low.astype(jnp.int32) + has_high.astype(jnp.int32)
-    )
+    gather_sends(0, tab_a)
 
     def copies_a(which):
         copies = []
@@ -351,27 +371,36 @@
 
     first_copies = copies_a(0)
     late_copies = copies_a(1)
+    pl.semaphore_wait(barrier, 2 + has_low.astype(jnp.int32) + has_high.astype(jnp.int32))
     start(first_copies)
+    announce(0, 1)
+
+    later = integrate(series, SECOND_HALF)
+    tab_b[...] = dot(traces[0:48], split_state(later))
+    gather_sends(1, tab_b)
     start(late_copies)
-
-    def peer_copies(src, dst, ss, rs):
-        return {
-            k: pltpu.make_async_remote_copy(
-                src_ref=src.at[k],
-                dst_ref=dst.at[k],
-                send_sem=ss.at[k],
-                recv_sem=rs.at[k],
-                device_id={"dom": lax.rem(d + k, n_dom)},
-                device_id_type=MESH,
-            )
-            for k in range(1, n_dom)
-        }
-
-    nearest = sorted(range(1, n_dom), key=lambda k: min(k, n_dom - k))
-    land_copies = peer_copies(land_out, land_in, ss_land, rs_land)
-    for k in nearest[::-1]:
-        land_copies[k].start()
-
+    pl.semaphore_wait(ready.at[0], 2)
+    announce(1, 2)
+
+    for i in range(2):
+
+        @pl.when(jnp.logical_not(comes[i]))
+        def _():
+            in_reg[:, i] = jnp.zeros(in_reg.shape[0:1] + in_reg.shape[2:], F32)
+
+        @pl.when(jnp.logical_not(comes[2 + i]))
+        def _():
+            in_dom[:, i] = jnp.zeros(in_dom.shape[0:1] + in_dom.shape[2:], F32)
+
+    for i in range(4):
+
+        @pl.when(jnp.logical_not(comes[i]))
+        def _():
+            in_fine[i] = jnp.zeros((16, 128), F32)
+
+    for i in (4, 6, 7, 8, 11, 12):
+        loads[i].wait()
+    tab_a[48:96] = dot(traces[48:96], early_split)
     stiff = slope_matrix(stiff_ref, 1.0)
     lift = lift_matrix(lift_ref)
     half_x = (-m1, m0 + m1, -m0)
@@ -446,6 +475,22 @@
         return volume + dot(lift, split_state(jnp.concatenate(parts, axis=0)))
 
     local_part(tab_a)
+    pl.semaphore_wait(ready.at[1], 2)
+    announce(2, 2)
+    nearest = sorted(range(1, n_dom), key=lambda k: min(k, n_dom - k))
+    def peer_copies(src, dst, ss, rs):
+        return {
+            k: pltpu.make_async_remote_copy(
+                src_ref=src.at[k],
+                dst_ref=dst.at[k],
+                send_sem=ss.at[k],
+                recv_sem=rs.at[k],
+                device_id={"dom": lax.rem(d + k, n_dom)},
+                device_id_type=MESH,
+            )
+            for k in range(1, n_dom)
+        }
+
     wait_recv(first_copies)
     remote_part(0, False)
     midway = state + increment(early_split, tab_a)
@@ -490,6 +535,36 @@
         )
     start(fine_copies)
 
+    lanes = iota((1, elems), 1)
+    offset = move_dom_ref[...] - d
+    offset = jnp.where(offset < 0, offset + n_dom, offset)
+    chosen = jnp.where(iota((16, elems), 0) == offset, 1.0, 0.0)
+    before = jnp.where(iota((elems, elems), 0) < iota((elems, elems), 1), 1.0, 0.0).astype(BF16)
+    rank = jnp.sum(chosen * dot(chosen.astype(BF16), before), axis=0, keepdims=True)
+    slots = n_dom * MIGRANTS
+    padded = 384 if slots <= 384 else 128 * (-(-slots // 128))
+    position = jnp.where(offset == 0, -1, offset * MIGRANTS + rank.astype(jnp.int32))
+    inverse = jnp.where(iota((padded, elems), 0) == position, 1.0, 0.0).astype(BF16)
+    place = move_slot_ref[...]
+    which_row = iota((8, elems), 0)
+    facts = jnp.where(
+        which_row == 0,
+        lanes >> 1,
+        jnp.where(
+            which_row == 1, lanes & 1, jnp.where(which_row == 2, place >> 1, place & 1)
+        ),
+    )
+    facts = jnp.where(which_row < 4, facts, 0).astype(F32).astype(BF16)
+    found = dot_nt(facts, inverse).astype(jnp.int32)
+    leaves = found[0:1] * 2 + found[1:2]
+    lands = found[2:3] * 2 + found[3:4]
+    for k in range(1, n_dom):
+        land_out[k] = lands[:, 128 * (k // 4) : 128 * (k // 4) + 128]
+
+    pl.semaphore_wait(ready.at[2], 2)
+    land_copies = peer_copies(land_out, land_in, ss_land, rs_land)
+    for k in nearest[::-1]:
+        land_copies[k].start()
     local_part(tab_c)
     wait_recv(late_copies)
     remote_part(1, True)
@@ -600,12 +675,30 @@
     def kernel(*refs):
         step_kernel(n_region, n_dom, elems, *refs)
 
+    given = (
+        jnp.transpose(water_state, (1, 0, 2)),
+        water_depth.reshape(1, elems),
+        metric,
+        jnp.transpose(diff_ops, (1, 0, 2)),
+        jnp.transpose(stiff_ops, (1, 0, 2)),
+        trace_ops,
+        jnp.transpose(lift_ops, (0, 2, 1)),
+        cluster.reshape(1, elems),
+        face_code,
+        send_region,
+        send_dom,
+        move_dom.reshape(1, elems),
+        move_slot.reshape(1, elems),
+    )
     result = pl.pallas_call(
         kernel,
-        out_shape=jax.ShapeDtypeStruct((NODES, 3, elems), F32),
-        in_specs=[vmem] * 13,
+        out_shape=pltpu.VMEM((NODES, 3, elems), F32),
+        in_specs=[pl.BlockSpec(memory_space=pl.ANY)] * 13,
         out_specs=vmem,
-        scratch_shapes=[
+        scratch_shapes=[pltpu.VMEM(x.shape, x.dtype) for x in given]
+        + [
+            dma((13,)),
+            pltpu.SemaphoreType.REGULAR((3,)),
             pltpu.VMEM((32, elems), F32),
             pltpu.VMEM((96, elems), F32),
             pltpu.VMEM((48, elems), F32),
@@ -634,21 +727,7 @@
         ],
         compiler_params=pltpu.CompilerParams(collective_id=0, has_side_effects=True),
         name="wave_step",
-    )(
-        jnp.transpose(water_state, (1, 0, 2)),
-        water_depth.reshape(1, elems),
-        metric,
-        jnp.transpose(diff_ops, (1, 0, 2)),
-        jnp.transpose(stiff_ops, (1, 0, 2)),
-        trace_ops,
-        jnp.transpose(lift_ops, (0, 2, 1)),
-        cluster.reshape(1, elems),
-        face_code,
-        send_region,
-        send_dom,
-        move_dom.reshape(1, elems),
-        move_slot.reshape(1, elems),
-    )
+    )(*given)
     return jnp.transpose(result, (1, 0, 2))
 
 

time: 34.5 us -> 34.6 us (level)
  Pallas kernels: 32.8 us -> 33.8 us
  local copies, waits for them, and re-layouts: 1.54 us -> 0.64 us
    pallas_call x1, Pallas kernels: 32.8 us -> 33.8 us  [shards(): pl.pallas_call(kernel, out_shape=pltpu.VMEM((NODES, 3, elems), F32), in_s...]
    unnamed x1, local copies, waits for them, and re-layouts: 1.54 us -> 0.64 us
where the time goes in v2:
time: 34.6 us; the launch traced here: 34.5 us
  Pallas kernels  33.8 us (98%)
  local copies, waits for them, and re-layouts  0.64 us (2%)
    pallas_call x1, Pallas kernels, shards(): pl.pallas_call(kernel, out_shape=pltpu.VMEM((NODES, 3, elems), F32), in_s...  33.8 us

profile of v2, /device:TPU:6, one launch (start us, length us, event | category | flops | bytes accessed | tf_op | source)
XLA Modules:
  0.0 34.5 jit_solution(13958878722489067025)
XLA Ops:
  0.0 33.8 %wave_step.1 = f32[10,3,512]{2,1,0:T(4,128)S(1)} custom-call(f32[10,3,512]{2,1,0:T(4,128)} %bitcast.10, f32[1,512]{1,0:T(1,128)} %bitcast.14, f32[4,512]{1,0:T(4,128)} %refs_2_.1, f32[10,2,10]{2,1,0:T(2,128)} %bitcast.11, f32[10,2,10]{2,1,0:T(2,128)} %bitcast.12, f32[3,4,10]{2,1,0:T(4,128)} %refs_5_.1, f32[3,4,10]{2,1,0:T(4,128)} %bitcast.13, ...), custom_call_target="tpu_custom_call" | custom-call | tf_op jit(solution)/shard_map/wave_step/pallas_call | solution.py:693
  33.8 0.6 %copy.15 = f32[3,10,512]{2,0,1:T(4,128)} copy(f32[3,10,512]{2,0,1:T(4,128)S(1)} %bitcast.9) | data formatting | bytes 122880

commit v3 on v2

--- a/solution.py
+++ b/solution.py
@@ -1,12 +1,12 @@
 import jax
 import jax.numpy as jnp
+import numpy as np
 from jax import lax
 from jax.experimental import pallas as pl
 from jax.experimental.pallas import tpu as pltpu
 from jax.sharding import PartitionSpec as P
 
 MESH = pl.DeviceIdType.MESH
-HIGHEST = lax.Precision.HIGHEST
 F32 = jnp.float32
 BF16 = jnp.bfloat16
 NODES = 10
@@ -15,28 +15,20 @@
 MIGRANTS = 32
 REG_FINE = 8
 DOM_FINE = 4
+EARLY_LOADS = (3, 5, 13, 14, 15, 0, 1, 2, 9, 10)
+LATE_LOADS = (4, 6, 7, 8, 11, 12, 16, 17, 18)
 
 
 def iota(shape, dim):
     return lax.broadcasted_iota(jnp.int32, shape, dim)
 
 
-def ones_where(mask):
-    return jnp.where(mask, 1.0, 0.0).astype(F32)
-
-
 def dot(a, b):
     return jnp.dot(a, b, preferred_element_type=F32)
 
 
-def exact(a, b):
-    return jnp.dot(a, b, preferred_element_type=F32, precision=HIGHEST)
-
-
-def dot_nt(a, b, precision=None):
-    return lax.dot_general(
-        a, b, (((1,), (1,)), ((), ())), preferred_element_type=F32, precision=precision
-    )
+def dot_nt(a, b):
+    return lax.dot_general(a, b, (((1,), (1,)), ((), ())), preferred_element_type=F32)
 
 
 def split_state(values):
@@ -45,84 +37,62 @@
     return jnp.concatenate([hi, lo, hi], axis=0)
 
 
-def split_matrix(wide, low_from):
-    hi = wide.astype(BF16).astype(F32)
-    lo = wide - hi
-    return jnp.where(iota(wide.shape, 1) >= low_from, lo, hi).astype(BF16)
-
-
-def var_of(row):
-    return (row >= NODES).astype(jnp.int32) + (row >= 2 * NODES).astype(jnp.int32)
-
-
-def state_columns(count):
-    column = iota((NODES, count), 1) & 31
-    node = column - NODES * var_of(column)
-    return ones_where((node == iota((NODES, count), 0)) & (column < 3 * NODES))
-
-
-def slope_matrix(ops_ref, sign):
-    rows, cols = 96, 96
-    row = iota((rows, NODES), 0)
-    local = jnp.where(row < 64, row & 31, row & 15)
-    node = local - NODES * var_of(local)
-    second = ((row >= 32) & (row < 64)) | (row >= 80)
-    valid = local < jnp.where(row < 64, 3 * NODES, NODES)
-    hit = (node == iota((rows, NODES), 1)) & valid
-    picked = exact(ones_where(hit & ~second), ops_ref[:, 0, :]) + exact(
-        ones_where(hit & second), ops_ref[:, 1, :]
-    )
-    wide = exact(picked, state_columns(cols)) * sign
-    row = iota((rows, cols), 0)
-    local = row & 31
-    source = jnp.where(row < 64, (local < NODES).astype(jnp.int32), 2)
-    column = iota((rows, cols), 1) & 31
-    wide = jnp.where(source == var_of(column), wide, 0.0)
-    return split_matrix(wide, 64)
-
-
-def trace_matrix(trace_ref):
-    rows, cols = 96, 96
-    row = iota((rows, 4), 0)
-    point = row & 3
-    point = jnp.where(row < 48, 3 - point, point)
-    face = (row >> 4) - jnp.where(row < 48, 0, 3)
-    picked = jnp.zeros((rows, NODES), F32)
-    for f in range(3):
-        pick = ones_where((point == iota((rows, 4), 1)) & (face == f))
-        picked = picked + exact(pick, trace_ref[f])
-    wide = exact(picked, state_columns(cols))
-    part = (iota((rows, cols), 0) >> 2) & 3
-    source = jnp.where(part == 3, 0, part)
-    column = iota((rows, cols), 1) & 31
-    wide = jnp.where(source == var_of(column), wide, 0.0)
-    return split_matrix(wide, 64)
-
-
-def lift_matrix(lift_ref):
-    rows, cols = 32, 288
-    row = iota((rows, NODES), 0)
-    node = row - NODES * var_of(row)
-    pick = ones_where((node == iota((rows, NODES), 1)) & (row < 3 * NODES))
-    wide = jnp.zeros((rows, cols), F32)
-    column = iota((4, cols), 1)
-    third = column - 96 * ((column >= 96).astype(jnp.int32) + (column >= 192).astype(jnp.int32))
-    for f in range(3):
-        points = dot_nt(pick, lift_ref[f], HIGHEST)
-        place = ones_where(((third >> 5) == f) & ((third & 3) == iota((4, cols), 0)))
-        wide = wide + exact(points, place)
-    column = iota((rows, cols), 1)
-    third = column - 96 * ((column >= 96).astype(jnp.int32) + (column >= 192).astype(jnp.int32))
-    jump = (third & 16) != 0
-    part = (third >> 2) & 3
-    var = var_of(iota((rows, cols), 0))
-    centre = (
-        ((var == 0) & ((part == 1) | (part == 2)))
-        | ((var == 1) & (part == 0))
-        | ((var == 2) & (part == 3))
-    )
-    factor = jnp.where(jump, ones_where(part == var), -ones_where(centre))
-    return split_matrix(wide * factor, 192)
+def pattern():
+    pick = np.zeros((192, 32), np.float32)
+    mask = np.zeros((192, 96), np.float32)
+    columns = np.zeros((2, 16, 96), np.float32)
+    for column in range(96):
+        third, at = divmod(column, 32)
+        if at < 3 * NODES:
+            columns[third // 2, at % NODES, column] = 1.0
+
+    def fill(row, source, var, sign):
+        pick[row, source] = 1.0
+        for third in range(3):
+            first = 32 * third + NODES * var
+            mask[row, first : first + NODES] = sign
+
+    for which in range(2):
+        for at in range(3 * NODES):
+            node, part = at % NODES, at // NODES
+            fill(32 * which + at, NODES * which + node, 1 if part == 0 else 0, -1.0)
+        for node in range(NODES):
+            fill(64 + 16 * which + node, NODES * which + node, 2, -1.0)
+    for order in range(2):
+        for face in range(3):
+            for at in range(16):
+                part, point = divmod(at, 4)
+                source = 2 * NODES + 4 * face + (point if order else 3 - point)
+                fill(96 + 48 * order + 16 * face + at, source, part % 3, 1.0)
+
+    nodes = np.zeros((32, 16), np.float32)
+    for row in range(3 * NODES):
+        nodes[row, row % NODES] = 1.0
+    places = np.zeros((2, 16, 288), np.float32)
+    signs = np.zeros((32, 288), np.float32)
+    for column in range(288):
+        third, rest = divmod(column, 96)
+        face, at = divmod(rest, 32)
+        jump, at = divmod(at, 16)
+        part, point = divmod(at, 4)
+        places[third // 2, 4 * face + point, column] = 1.0
+        for row in range(3 * NODES):
+            var = row // NODES
+            if jump:
+                signs[row, column] = 1.0 if part == var else 0.0
+            else:
+                signs[row, column] = -1.0 if part in ((1, 2), (0,), (3,))[var] else 0.0
+    return [jnp.asarray(x, BF16) for x in (pick, mask, columns, nodes, places, signs)]
+
+
+def halves(values):
+    hi = values.astype(BF16)
+    return hi, (values - hi.astype(F32)).astype(BF16)
+
+
+def spread_columns(values, columns_ref):
+    hi, lo = halves(values)
+    return (dot(hi, columns_ref[0]) + dot(lo, columns_ref[1])).astype(BF16)
 
 
 def combine(slopes, alpha):
@@ -157,6 +127,12 @@
     send_dom_ref,
     move_dom_ref,
     move_slot_ref,
+    pick_ref,
+    mask_ref,
+    columns_ref,
+    nodes_ref,
+    places_ref,
+    signs_ref,
     out_ref,
     *scratch,
 ):
@@ -174,6 +150,12 @@
         send_dom_ref,
         move_dom_ref,
         move_slot_ref,
+        pick_ref,
+        mask_ref,
+        columns_ref,
+        nodes_ref,
+        places_ref,
+        signs_ref,
     )
     step_body(
         n_region, n_dom, elems, hbm_refs, out_ref, scratch[: len(hbm_refs)], *scratch[len(hbm_refs) :]
@@ -189,6 +171,9 @@
     local_refs,
     in_sem,
     ready,
+    first_ops,
+    second_ops,
+    lift_ops,
     dense,
     tab_a,
     tab_b,
@@ -239,7 +224,7 @@
     def ring(k):
         return {"dom": lax.rem(d + k + n_dom, n_dom)}
 
-    for i in (0, 1, 2, 3, 5, 9, 10):
+    for i in EARLY_LOADS:
         loads[i].start()
     for exists, device, _, _ in sides[:2]:
 
@@ -249,7 +234,7 @@
 
     for k in (1, -1):
         pl.semaphore_signal(barrier, inc=1, device_id=ring(k), device_id_type=MESH)
-    for i in (4, 6, 7, 8, 11, 12):
+    for i in LATE_LOADS:
         loads[i].start()
 
     def announce(stage, reach):
@@ -272,8 +257,17 @@
         send_dom_ref,
         move_dom_ref,
         move_slot_ref,
+        pick_ref,
+        mask_ref,
+        columns_ref,
+        nodes_ref,
+        places_ref,
+        signs_ref,
     ) = local_refs
-    for i in (0, 1, 2, 3, 5, 9, 10):
+    first_ops[...] = jnp.zeros((32, 16), F32)
+    second_ops[...] = jnp.zeros((32, 16), F32)
+    lift_ops[...] = jnp.zeros((16, 16), F32)
+    for i in EARLY_LOADS:
         loads[i].wait()
 
     dense[30:32, :] = jnp.zeros((2, elems), F32)
@@ -291,8 +285,13 @@
     a4 = jnp.where(top, m3, 0.0)
     alpha = (a1, a2, a3, a4)
 
-    slope = slope_matrix(diff_ref, -1.0)
-    traces = trace_matrix(trace_ref)
+    for a in range(2):
+        first_ops[NODES * a : NODES * (a + 1), 0:NODES] = diff_ref[:, a, :]
+    for f in range(3):
+        first_ops[2 * NODES + 4 * f : 2 * NODES + 4 * f + 4, 0:NODES] = trace_ref[f]
+    wide = dot(pick_ref[...], spread_columns(first_ops[...], columns_ref)).astype(BF16)
+    wide = wide * mask_ref[...]
+    slope, traces = wide[0:96], wide[96:192]
 
     def series_of(values):
         series = [values]
@@ -379,8 +378,6 @@
     tab_b[...] = dot(traces[0:48], split_state(later))
     gather_sends(1, tab_b)
     start(late_copies)
-    pl.semaphore_wait(ready.at[0], 2)
-    announce(1, 2)
 
     for i in range(2):
 
@@ -398,11 +395,19 @@
         def _():
             in_fine[i] = jnp.zeros((16, 128), F32)
 
-    for i in (4, 6, 7, 8, 11, 12):
+    for i in LATE_LOADS:
         loads[i].wait()
     tab_a[48:96] = dot(traces[48:96], early_split)
-    stiff = slope_matrix(stiff_ref, 1.0)
-    lift = lift_matrix(lift_ref)
+    for a in range(2):
+        second_ops[NODES * a : NODES * (a + 1), 0:NODES] = stiff_ref[:, a, :]
+    stiff = dot(pick_ref[0:96], spread_columns(second_ops[...], columns_ref)).astype(BF16)
+    stiff = -(stiff * mask_ref[0:96])
+    for f in range(3):
+        lift_ops[4 * f : 4 * f + 4, 0:NODES] = lift_ref[f]
+    hi, lo = halves(lift_ops[...])
+    lift = dot(dot_nt(nodes_ref[...], hi).astype(BF16), places_ref[0])
+    lift = lift + dot(dot_nt(nodes_ref[...], lo).astype(BF16), places_ref[1])
+    lift = lift.astype(BF16) * signs_ref[...]
     half_x = (-m1, m0 + m1, -m0)
     half_y = (-m3, m2 + m3, -m2)
     root = jnp.sqrt(depth)
@@ -432,7 +437,7 @@
                 wall = mirror * table[48 + 16 * f : 64 + 16 * f, 128 * b : 128 * b + 128]
                 beyond[f, b] = pick_columns(source(table), own, code >> 7, code & 127, wall)
 
-    def remote_part(which, fine):
+    def remote_part(which):
         def load(k):
             k = k - 3 * blocks
             if k < 4:
@@ -475,8 +480,8 @@
         return volume + dot(lift, split_state(jnp.concatenate(parts, axis=0)))
 
     local_part(tab_a)
-    pl.semaphore_wait(ready.at[1], 2)
-    announce(2, 2)
+    pl.semaphore_wait(ready.at[0], 2)
+    announce(1, 2)
     nearest = sorted(range(1, n_dom), key=lambda k: min(k, n_dom - k))
     def peer_copies(src, dst, ss, rs):
         return {
@@ -492,12 +497,12 @@
         }
 
     wait_recv(first_copies)
-    remote_part(0, False)
+    remote_part(0)
     midway = state + increment(early_split, tab_a)
     fine = integrate(series_of(midway), FIRST_HALF)
     second = jnp.where(cluster_ref[...] == 0, fine, later)
     second_split = split_state(second)
-    tab_c[...] = dot(traces, second_split)
+    tab_c[0:48] = dot(traces[0:48], second_split)
 
     lane = iota((1, 128), 1)
     wanted = jnp.where(
@@ -534,6 +539,8 @@
             )
         )
     start(fine_copies)
+    pl.semaphore_wait(ready.at[1], 2)
+    announce(2, 2)
 
     lanes = iota((1, elems), 1)
     offset = move_dom_ref[...] - d
@@ -561,31 +568,20 @@
     for k in range(1, n_dom):
         land_out[k] = lands[:, 128 * (k // 4) : 128 * (k // 4) + 128]
 
+    tab_c[48:96] = dot(traces[48:96], second_split)
+    local_part(tab_c)
+    wait_recv(late_copies)
+    remote_part(1)
+    columns = {}
+    for f in range(3):
+        for b in range(blocks):
+            columns[f, b] = fine_column(code_of(f, b))
+            beyond[f, b] = jnp.where(columns[f, b] >= 0, 0.0, beyond[f, b])
+    dense[...] = midway + increment(second_split, tab_c)
     pl.semaphore_wait(ready.at[2], 2)
     land_copies = peer_copies(land_out, land_in, ss_land, rs_land)
     for k in nearest[::-1]:
         land_copies[k].start()
-    local_part(tab_c)
-    wait_recv(late_copies)
-    remote_part(1, True)
-    for k in range(1, n_dom):
-        land_copies[k].wait_recv()
-    kk = iota((1, 128), 1)
-    stack = []
-    for q in range(padded // 128):
-        row_q = jnp.full((1, 128), -1, jnp.int32)
-        for k in range(4 * q, min(4 * q + 4, n_dom)):
-            if k > 0:
-                row_q = jnp.where((kk >> 5) == (k & 3), land_in[k], row_q)
-        stack.append(row_q)
-    places = jnp.concatenate(stack, axis=1)
-    comes_here = jnp.where(iota((elems, padded), 0) == places, 1.0, 0.0).astype(BF16)
-    column = iota((8, padded), 1)
-    row8 = iota((8, padded), 0)
-    facts = jnp.where(row8 == 0, column >> 1, jnp.where(row8 == 1, column & 1, 1))
-    found = dot_nt(facts.astype(F32).astype(BF16), comes_here).astype(jnp.int32)
-    origin = jnp.where(found[2:3] > 0, found[0:1] * 2 + found[1:2], -1)
-
     wait_recv(fine_copies)
     lane16 = iota((16, 128), 1)
     fresh = jnp.where(
@@ -597,12 +593,16 @@
             jnp.where(lane16 < 2 * REG_FINE + DOM_FINE, in_fine[2], in_fine[3]),
         ),
     )
+    parts = []
     for f in range(3):
+        late = []
         for b in range(blocks):
-            column = fine_column(code_of(f, b))
-            found = jnp.take_along_axis(fresh, column & 127, axis=1)
-            beyond[f, b] = jnp.where(column >= 0, found, beyond[f, b])
-    dense[...] = midway + increment(second_split, tab_c)
+            found = jnp.take_along_axis(fresh, columns[f, b] & 127, axis=1)
+            late.append(jnp.where(columns[f, b] >= 0, found, 0.0))
+        late = jnp.concatenate(late, axis=1)
+        parts.append(centre_by[f] * late)
+        parts.append(jump_by[f] * late)
+    dense[...] = dense[...] + dot(lift, split_state(jnp.concatenate(parts, axis=0)))
 
     def cell(g, b):
         return dense[8 * g : 8 * g + 8, 128 * b : 128 * b + 128]
@@ -626,6 +626,24 @@
             tile = jnp.where(group == g, moved, tile)
         tile_out[k] = tile
         tile_copies[k].start()
+
+    for k in range(1, n_dom):
+        land_copies[k].wait_recv()
+    kk = iota((1, 128), 1)
+    stack = []
+    for q in range(padded // 128):
+        row_q = jnp.full((1, 128), -1, jnp.int32)
+        for k in range(4 * q, min(4 * q + 4, n_dom)):
+            if k > 0:
+                row_q = jnp.where((kk >> 5) == (k & 3), land_in[k], row_q)
+        stack.append(row_q)
+    places = jnp.concatenate(stack, axis=1)
+    comes_here = jnp.where(iota((elems, padded), 0) == places, 1.0, 0.0).astype(BF16)
+    column = iota((8, padded), 1)
+    row8 = iota((8, padded), 0)
+    facts = jnp.where(row8 == 0, column >> 1, jnp.where(row8 == 1, column & 1, 1))
+    found = dot_nt(facts.astype(F32).astype(BF16), comes_here).astype(jnp.int32)
+    origin = jnp.where(found[2:3] > 0, found[0:1] * 2 + found[1:2], -1)
 
     result = {(g, b): cell(g, b) for g in range(4) for b in range(blocks)}
     for k in nearest:
@@ -689,16 +707,20 @@
         send_dom,
         move_dom.reshape(1, elems),
         move_slot.reshape(1, elems),
+        *pattern(),
     )
     result = pl.pallas_call(
         kernel,
         out_shape=pltpu.VMEM((NODES, 3, elems), F32),
-        in_specs=[pl.BlockSpec(memory_space=pl.ANY)] * 13,
+        in_specs=[pl.BlockSpec(memory_space=pl.ANY)] * len(given),
         out_specs=vmem,
         scratch_shapes=[pltpu.VMEM(x.shape, x.dtype) for x in given]
         + [
-            dma((13,)),
+            dma((len(given),)),
             pltpu.SemaphoreType.REGULAR((3,)),
+            pltpu.VMEM((32, 16), F32),
+            pltpu.VMEM((32, 16), F32),
+            pltpu.VMEM((16, 16), F32),
             pltpu.VMEM((32, elems), F32),
             pltpu.VMEM((96, elems), F32),
             pltpu.VMEM((48, elems), F32),

time: 34.6 us -> 30.1 us (0.87)
  Pallas kernels: 33.8 us -> 29.3 us
    pallas_call x1, Pallas kernels: 33.8 us -> 29.3 us  [shards(): pl.pallas_call(kernel, out_shape=pltpu.VMEM((NODES, 3, elems), F32), in_s...]
where the time goes in v3:
time: 30.1 us; the launch traced here: 29.9 us
  Pallas kernels  29.3 us (97%)
  local copies, waits for them, and re-layouts  0.64 us (2%)
    pallas_call x1, Pallas kernels, shards(): pl.pallas_call(kernel, out_shape=pltpu.VMEM((NODES, 3, elems), F32), in_s...  29.3 us
    unnamed x1, local copies, waits for them, and re-layouts  0.64 us

profile of v3, /device:TPU:6, one launch (start us, length us, event | category | flops | bytes accessed | tf_op | source)
XLA Modules:
  0.0 29.9 jit_solution(7134078843290200259)
XLA Ops:
  0.0 29.3 %wave_step.1 = f32[10,3,512]{2,1,0:T(4,128)S(1)} custom-call(f32[10,3,512]{2,1,0:T(4,128)} %bitcast.10, f32[1,512]{1,0:T(1,128)} %bitcast.14, f32[4,512]{1,0:T(4,128)} %refs_2_.1, f32[10,2,10]{2,1,0:T(2,128)} %bitcast.11, f32[10,2,10]{2,1,0:T(2,128)} %bitcast.12, f32[3,4,10]{2,1,0:T(4,128)} %refs_5_.1, f32[3,4,10]{2,1,0:T(4,128)} %bitcast.13, ...), custom_call_target="tpu_custom_call" | custom-call | tf_op jit(solution)/shard_map/wave_step/pallas_call | solution.py:712
  29.3 0.6 %copy.21 = f32[3,10,512]{2,0,1:T(4,128)} copy(f32[3,10,512]{2,0,1:T(4,128)S(1)} %bitcast.9) | data formatting | bytes 122880

commit v4 on v3

--- a/solution.py
+++ b/solution.py
@@ -15,6 +15,7 @@
 MIGRANTS = 32
 REG_FINE = 8
 DOM_FINE = 4
+FINE_LANES = 32
 EARLY_LOADS = (3, 5, 13, 14, 15, 0, 1, 2, 9, 10)
 LATE_LOADS = (4, 6, 7, 8, 11, 12, 16, 17, 18)
 
@@ -322,19 +323,21 @@
 
     own = range(3 * blocks)
 
-    def gather_sends(which, table):
-        for lane_row in range(2):
-            for b in range(2):
-                index = spread(send_reg_ref[lane_row : lane_row + 1, 128 * b : 128 * b + 128])
-                out_reg[which, lane_row, b] = pick_columns(
+    def gather_sends(which, table, copies):
+        for i, (exists, _, copy) in enumerate(copies):
+            lane_row = sides[i][2]
+            if i < 2:
+                for b in range(2):
+                    index = spread(send_reg_ref[lane_row : lane_row + 1, 128 * b : 128 * b + 128])
+                    out_reg[which, lane_row, b] = pick_columns(
+                        source(table), own, index >> 7, index & 127, jnp.zeros((16, 128), F32)
+                    )
+            else:
+                index = spread(send_dom_ref[lane_row : lane_row + 1, :])
+                out_dom[which, lane_row] = pick_columns(
                     source(table), own, index >> 7, index & 127, jnp.zeros((16, 128), F32)
                 )
-            index = spread(send_dom_ref[lane_row : lane_row + 1, :])
-            out_dom[which, lane_row] = pick_columns(
-                source(table), own, index >> 7, index & 127, jnp.zeros((16, 128), F32)
-            )
-
-    gather_sends(0, tab_a)
+            pl.when(exists)(copy.start)
 
     def copies_a(which):
         copies = []
@@ -371,13 +374,12 @@
     first_copies = copies_a(0)
     late_copies = copies_a(1)
     pl.semaphore_wait(barrier, 2 + has_low.astype(jnp.int32) + has_high.astype(jnp.int32))
-    start(first_copies)
     announce(0, 1)
+    gather_sends(0, tab_a, first_copies)
 
     later = integrate(series, SECOND_HALF)
     tab_b[...] = dot(traces[0:48], split_state(later))
-    gather_sends(1, tab_b)
-    start(late_copies)
+    gather_sends(1, tab_b, late_copies)
 
     for i in range(2):
 
@@ -393,7 +395,7 @@
 
         @pl.when(jnp.logical_not(comes[i]))
         def _():
-            in_fine[i] = jnp.zeros((16, 128), F32)
+            in_fine[i] = jnp.zeros((8, 128), F32)
 
     for i in LATE_LOADS:
         loads[i].wait()
@@ -519,9 +521,11 @@
         ),
     )
     wanted = spread(wanted)
-    out_fine[...] = pick_columns(
+    block = pick_columns(
         source(tab_c), own, wanted >> 7, wanted & 127, jnp.zeros((16, 128), F32)
     )
+    lane8 = iota((8, 128), 1)
+    out_fine[...] = jnp.where(lane8 < FINE_LANES, block[0:8], pltpu.roll(block[8:16], FINE_LANES, 1))
     fine_copies = []
     for i, (exists, device, _, at) in enumerate(sides):
         fine_copies.append(
@@ -583,21 +587,24 @@
     for k in nearest[::-1]:
         land_copies[k].start()
     wait_recv(fine_copies)
-    lane16 = iota((16, 128), 1)
+    at = lane8 & (FINE_LANES - 1)
     fresh = jnp.where(
-        lane16 < REG_FINE,
+        at < REG_FINE,
         in_fine[0],
         jnp.where(
-            lane16 < 2 * REG_FINE,
+            at < 2 * REG_FINE,
             in_fine[1],
-            jnp.where(lane16 < 2 * REG_FINE + DOM_FINE, in_fine[2], in_fine[3]),
+            jnp.where(at < 2 * REG_FINE + DOM_FINE, in_fine[2], in_fine[3]),
         ),
     )
     parts = []
     for f in range(3):
         late = []
         for b in range(blocks):
-            found = jnp.take_along_axis(fresh, columns[f, b] & 127, axis=1)
+            column = columns[f, b][0:8] & (FINE_LANES - 1)
+            low = jnp.take_along_axis(fresh, column, axis=1)
+            high = jnp.take_along_axis(fresh, column + FINE_LANES, axis=1)
+            found = jnp.concatenate([low, high], axis=0)
             late.append(jnp.where(columns[f, b] >= 0, found, 0.0))
         late = jnp.concatenate(late, axis=1)
         parts.append(centre_by[f] * late)
@@ -625,7 +632,19 @@
                 moved = pltpu.roll(moved, shift, 1)
             tile = jnp.where(group == g, moved, tile)
         tile_out[k] = tile
-        tile_copies[k].start()
+    for target in range(n_dom):
+
+        @pl.when(target != d)
+        def _():
+            k = lax.rem(target - d + n_dom, n_dom)
+            pltpu.make_async_remote_copy(
+                src_ref=tile_out.at[k],
+                dst_ref=tile_in.at[k],
+                send_sem=ss_tile.at[k],
+                recv_sem=rs_tile.at[k],
+                device_id={"dom": target},
+                device_id_type=MESH,
+            ).start()
 
     for k in range(1, n_dom):
         land_copies[k].wait_recv()
@@ -645,6 +664,12 @@
     found = dot_nt(facts.astype(F32).astype(BF16), comes_here).astype(jnp.int32)
     origin = jnp.where(found[2:3] > 0, found[0:1] * 2 + found[1:2], -1)
 
+    wait_send(first_copies)
+    wait_send(late_copies)
+    wait_send(fine_copies)
+    for k in range(1, n_dom):
+        land_copies[k].wait_send()
+        tile_copies[k].wait_send()
     result = {(g, b): cell(g, b) for g in range(4) for b in range(blocks)}
     for k in nearest:
         tile_copies[k].wait_recv()
@@ -660,13 +685,6 @@
             dense[8 * g : 8 * g + 8, 128 * b : 128 * b + 128] = result[g, b]
     for v in range(3):
         out_ref[:, v, :] = dense[NODES * v : NODES * (v + 1), :]
-
-    wait_send(first_copies)
-    wait_send(late_copies)
-    wait_send(fine_copies)
-    for k in range(1, n_dom):
-        land_copies[k].wait_send()
-        tile_copies[k].wait_send()
 
 
 def shards(n_region, n_dom, *args):
@@ -730,8 +748,8 @@
             pltpu.VMEM((2, 2, 16, 128), F32),
             pltpu.VMEM((2, 2, 2, 16, 128), F32),
             pltpu.VMEM((2, 2, 16, 128), F32),
-            pltpu.VMEM((16, 128), F32),
-            pltpu.VMEM((4, 16, 128), F32),
+            pltpu.VMEM((8, 128), F32),
+            pltpu.VMEM((4, 8, 128), F32),
             pltpu.VMEM((n_dom, 1, 128), jnp.int32),
             pltpu.VMEM((n_dom, 1, 128), jnp.int32),
             pltpu.VMEM((n_dom, 8, 128), F32),

time: 30.1 us -> 30.1 us (level)
  no operation moved by 1% of the time
where the time goes in v4:
time: 30.1 us; the launch traced here: 29.9 us
  Pallas kernels  29.3 us (97%)
  local copies, waits for them, and re-layouts  0.64 us (2%)
    pallas_call x1, Pallas kernels, shards(): pl.pallas_call(kernel, out_shape=pltpu.VMEM((NODES, 3, elems), F32), in_s...  29.3 us
    unnamed x1, local copies, waits for them, and re-layouts  0.64 us

profile of v4, /device:TPU:6, one launch (start us, length us, event | category | flops | bytes accessed | tf_op | source)
XLA Modules:
  0.0 29.9 jit_solution(8225055045765234377)
XLA Ops:
  0.0 29.3 %wave_step.1 = f32[10,3,512]{2,1,0:T(4,128)S(1)} custom-call(f32[10,3,512]{2,1,0:T(4,128)} %bitcast.10, f32[1,512]{1,0:T(1,128)} %bitcast.14, f32[4,512]{1,0:T(4,128)} %refs_2_.1, f32[10,2,10]{2,1,0:T(2,128)} %bitcast.11, f32[10,2,10]{2,1,0:T(2,128)} %bitcast.12, f32[3,4,10]{2,1,0:T(4,128)} %refs_5_.1, f32[3,4,10]{2,1,0:T(4,128)} %bitcast.13, ...), custom_call_target="tpu_custom_call" | custom-call | tf_op jit(solution)/shard_map/wave_step/pallas_call | solution.py:730
  29.3 0.6 %copy.21 = f32[3,10,512]{2,0,1:T(4,128)} copy(f32[3,10,512]{2,0,1:T(4,128)S(1)} %bitcast.9) | data formatting | bytes 122880

commit v5 on v4

--- a/solution.py
+++ b/solution.py
@@ -101,6 +101,39 @@
     both = a1 * slopes[0:32] + a2 * slopes[32:64]
     top = a3 * slopes[64:80] + a4 * slopes[80:96]
     return jnp.concatenate([both[0:16] + top, both[16:32]], axis=0)
+
+
+def alpha_of(depth, m0, m1, m2, m3):
+    row = iota((32, depth.shape[1]), 0)
+    top = row[0:16] < NODES
+    return (
+        jnp.where(row < 10, m0, jnp.where(row < 20, depth * m0, depth * m2)),
+        jnp.where(row < 10, m1, jnp.where(row < 20, depth * m1, depth * m3)),
+        jnp.where(top, m2, 0.0),
+        jnp.where(top, m3, 0.0),
+    )
+
+
+def flux_factors(depth, m0, m1, m2, m3):
+    rows = iota((16, depth.shape[1]), 0)
+    root = jnp.sqrt(depth)
+    factors = []
+    for hx, hy in ((-m1, -m3), (m0 + m1, m2 + m3), (-m0, -m2)):
+        centre = jnp.where(
+            rows < 4,
+            depth * hx,
+            jnp.where(rows < 8, hx, jnp.where(rows < 12, hy, depth * hy)),
+        )
+        factors.append((centre, root * jnp.sqrt(hx * hx + hy * hy)))
+    return factors
+
+
+def lifted(lift, factors, sums, differences):
+    parts = []
+    for (centre, jump), added, taken in zip(factors, sums, differences):
+        parts.append(centre * added)
+        parts.append(jump * taken)
+    return dot(lift, split_state(jnp.concatenate(parts, axis=0)))
 
 
 def pick_columns(load, sources, block, lane, start):
@@ -176,6 +209,8 @@
     second_ops,
     lift_ops,
     dense,
+    base,
+    geometry,
     tab_a,
     tab_b,
     tab_c,
@@ -278,13 +313,7 @@
     depth = depth_ref[...]
     m0, m1, m2, m3 = (metric_ref[i : i + 1, :] for i in range(4))
 
-    row = iota((32, elems), 0)
-    a1 = jnp.where(row < 10, m0, jnp.where(row < 20, depth * m0, depth * m2))
-    a2 = jnp.where(row < 10, m1, jnp.where(row < 20, depth * m1, depth * m3))
-    top = row[0:16] < 10
-    a3 = jnp.where(top, m2, 0.0)
-    a4 = jnp.where(top, m3, 0.0)
-    alpha = (a1, a2, a3, a4)
+    alpha = alpha_of(depth, m0, m1, m2, m3)
 
     for a in range(2):
         first_ops[NODES * a : NODES * (a + 1), 0:NODES] = diff_ref[:, a, :]
@@ -294,7 +323,7 @@
     wide = wide * mask_ref[...]
     slope, traces = wide[0:96], wide[96:192]
 
-    def series_of(values):
+    def series_of(values, alpha):
         series = [values]
         for _ in range(3):
             series.append(combine(dot(slope, split_state(series[-1])), alpha))
@@ -306,7 +335,7 @@
             summed = summed + factor * member
         return summed
 
-    series = series_of(state)
+    series = series_of(state, alpha)
     early = integrate(series, FIRST_HALF)
     early_split = split_state(early)
     tab_a[0:48] = dot(traces[0:48], early_split)
@@ -381,6 +410,7 @@
     tab_b[...] = dot(traces[0:48], split_state(later))
     gather_sends(1, tab_b, late_copies)
 
+    tile_in[0] = jnp.zeros((8, 128), F32)
     for i in range(2):
 
         @pl.when(jnp.logical_not(comes[i]))
@@ -410,24 +440,12 @@
     lift = dot(dot_nt(nodes_ref[...], hi).astype(BF16), places_ref[0])
     lift = lift + dot(dot_nt(nodes_ref[...], lo).astype(BF16), places_ref[1])
     lift = lift.astype(BF16) * signs_ref[...]
-    half_x = (-m1, m0 + m1, -m0)
-    half_y = (-m3, m2 + m3, -m2)
-    root = jnp.sqrt(depth)
-    rows16 = iota((16, elems), 0)
-    centre_by, jump_by = [], []
-    for f in range(3):
-        hx, hy = half_x[f], half_y[f]
-        centre_by.append(
-            jnp.where(
-                rows16 < 4,
-                depth * hx,
-                jnp.where(rows16 < 8, hx, jnp.where(rows16 < 12, hy, depth * hy)),
-            )
-        )
-        jump_by.append(root * jnp.sqrt(hx * hx + hy * hy))
+    factors = flux_factors(depth, m0, m1, m2, m3)
     mirror = jnp.where((iota((16, 128), 0) >= 4) & (iota((16, 128), 0) < 12), -1.0, 1.0)
     first_code = 3 * elems
     regional = 2 * send_reg_ref.shape[1]
+    wall_code = first_code + regional + 2 * send_dom_ref.shape[1]
+    remote = range(3 * blocks, 3 * blocks + 6)
 
     def code_of(f, b):
         return spread(code_ref[f : f + 1, 128 * b : 128 * b + 128])
@@ -437,25 +455,19 @@
             for b in range(blocks):
                 code = code_of(f, b)
                 wall = mirror * table[48 + 16 * f : 64 + 16 * f, 128 * b : 128 * b + 128]
+                wall = jnp.where(code == wall_code, wall, 0.0)
                 beyond[f, b] = pick_columns(source(table), own, code >> 7, code & 127, wall)
 
-    def remote_part(which):
-        def load(k):
-            k = k - 3 * blocks
-            if k < 4:
-                return in_reg[which, k // 2, k % 2]
-            return in_dom[which, k - 4]
-
-        for f in range(3):
-            for b in range(blocks):
-                code = code_of(f, b)
-                beyond[f, b] = pick_columns(
-                    load,
-                    range(3 * blocks, 3 * blocks + 6),
-                    code >> 7,
-                    code & 127,
-                    beyond[f, b],
-                )
+    def increment(values_split, table):
+        volume = combine(dot(stiff, values_split), alpha)
+        outside = [jnp.concatenate([beyond[f, b] for b in range(blocks)], axis=1) for f in range(3)]
+        inside = [table[48 + 16 * f : 64 + 16 * f, :] for f in range(3)]
+        return volume + lifted(
+            lift,
+            factors,
+            [x + y for x, y in zip(outside, inside)],
+            [x - y for x, y in zip(outside, inside)],
+        )
 
     def fine_column(code):
         slot = code - first_code
@@ -471,20 +483,12 @@
             from_reg,
         )
 
-    def increment(values_split, table):
-        volume = combine(dot(stiff, values_split), alpha)
-        parts = []
-        for f in range(3):
-            outside = jnp.concatenate([beyond[f, b] for b in range(blocks)], axis=1)
-            inside = table[48 + 16 * f : 64 + 16 * f, :]
-            parts.append(centre_by[f] * (outside + inside))
-            parts.append(jump_by[f] * (outside - inside))
-        return volume + dot(lift, split_state(jnp.concatenate(parts, axis=0)))
-
     local_part(tab_a)
+    base[...] = state + increment(early_split, tab_a)
     pl.semaphore_wait(ready.at[0], 2)
     announce(1, 2)
     nearest = sorted(range(1, n_dom), key=lambda k: min(k, n_dom - k))
+
     def peer_copies(src, dst, ss, rs):
         return {
             k: pltpu.make_async_remote_copy(
@@ -498,13 +502,63 @@
             for k in range(1, n_dom)
         }
 
-    wait_recv(first_copies)
-    remote_part(0)
-    midway = state + increment(early_split, tab_a)
-    fine = integrate(series_of(midway), FIRST_HALF)
-    second = jnp.where(cluster_ref[...] == 0, fine, later)
-    second_split = split_state(second)
-    tab_c[0:48] = dot(traces[0:48], second_split)
+    lanes = iota((1, elems), 1)
+    offset = move_dom_ref[...] - d
+    offset = jnp.where(offset < 0, offset + n_dom, offset)
+    fine_row = 15
+    is_fine = cluster_ref[...] == 0
+    kind = iota((16, elems), 0)
+    chosen = jnp.where(kind == offset, 1.0, 0.0)
+    chosen = jnp.where(kind == fine_row, jnp.where(is_fine, 1.0, 0.0), chosen)
+    before = jnp.where(iota((elems, elems), 0) < iota((elems, elems), 1), 1.0, 0.0).astype(BF16)
+    ranks = dot(chosen.astype(BF16), before)
+    rank = jnp.sum(jnp.where(kind < fine_row, chosen * ranks, 0.0), axis=0, keepdims=True)
+    fine_rank = ranks[fine_row:].astype(jnp.int32)
+    fine_position = jnp.where(is_fine, fine_rank, -1)
+    slots = n_dom * MIGRANTS
+    padded = 384 if slots <= 384 else 128 * (-(-slots // 128))
+    position = jnp.where(offset == 0, -1, offset * MIGRANTS + rank.astype(jnp.int32))
+    inverse = jnp.concatenate(
+        [
+            jnp.where(iota((padded, elems), 0) == position, 1.0, 0.0),
+            jnp.where(iota((128, elems), 0) == fine_position, 1.0, 0.0),
+        ],
+        axis=0,
+    ).astype(BF16)
+    place = move_slot_ref[...]
+    which_row = iota((8, elems), 0)
+    facts = jnp.where(
+        which_row == 0,
+        lanes >> 1,
+        jnp.where(
+            which_row == 1, lanes & 1, jnp.where(which_row == 2, place >> 1, place & 1)
+        ),
+    )
+    facts = jnp.where(which_row < 4, facts, 0).astype(F32).astype(BF16)
+    found = dot_nt(facts, inverse).astype(jnp.int32)
+    leaves = found[0:1] * 2 + found[1:2]
+    lands = found[2:3] * 2 + found[3:4]
+    fine_at = leaves[:, padded : padded + 128]
+    for k in range(1, n_dom):
+        land_out[k] = lands[:, 128 * (k // 4) : 128 * (k // 4) + 128]
+
+    geometry[0:1] = depth
+    geometry[1:5] = metric_ref[...]
+    geometry[5:8] = code_ref[...].astype(F32)
+
+    def squeeze(load, index):
+        index = jnp.broadcast_to(index, (8, 128))
+        return pick_columns(load, range(blocks), index >> 7, index & 127, jnp.zeros((8, 128), F32))
+
+    def block_of(ref, g):
+        return lambda b: ref[8 * g : 8 * g + 8, 128 * b : 128 * b + 128]
+
+    fine_base = jnp.concatenate([squeeze(block_of(base, g), fine_at) for g in range(4)], axis=0)
+    facts = squeeze(block_of(geometry, 0), fine_at)
+    fine_geometry = [facts[i : i + 1] for i in range(5)]
+    fine_alpha = alpha_of(*fine_geometry)
+    fine_factors = flux_factors(*fine_geometry)
+    fine_codes = [spread(facts[5 + f : 6 + f].astype(jnp.int32)) for f in range(3)]
 
     lane = iota((1, 128), 1)
     wanted = jnp.where(
@@ -520,10 +574,32 @@
             ),
         ),
     )
-    wanted = spread(wanted)
-    block = pick_columns(
-        source(tab_c), own, wanted >> 7, wanted & 127, jnp.zeros((16, 128), F32)
-    )
+    wanted_face = (wanted >= elems).astype(jnp.int32) + (wanted >= 2 * elems).astype(jnp.int32)
+    wanted_face = spread(wanted_face)
+    rank_rows = jnp.broadcast_to(fine_rank.astype(F32), (8, elems))
+    wanted_at = squeeze(
+        lambda b: rank_rows[:, 128 * b : 128 * b + 128], wanted - elems * wanted_face[0:1]
+    ).astype(jnp.int32)
+    wanted_at = spread(wanted_at[0:1]) & 127
+
+    wait_recv(first_copies)
+
+    def early_slot(k):
+        k = k - 3 * blocks
+        return in_reg[0, k // 2, k % 2] if k < 4 else in_dom[0, k - 4]
+
+    outer = [
+        pick_columns(early_slot, remote, code >> 7, code & 127, jnp.zeros((16, 128), F32))
+        for code in fine_codes
+    ]
+    fine_midway = fine_base + lifted(lift, fine_factors, outer, outer)
+    fine = integrate(series_of(fine_midway, fine_alpha), FIRST_HALF)
+    fine_table = dot(traces[0:48], split_state(fine))
+
+    block = jnp.zeros((16, 128), F32)
+    for f in range(3):
+        found = jnp.take_along_axis(fine_table[16 * f : 16 * f + 16], wanted_at, axis=1)
+        block = jnp.where(wanted_face == f, found, block)
     lane8 = iota((8, 128), 1)
     out_fine[...] = jnp.where(lane8 < FINE_LANES, block[0:8], pltpu.roll(block[8:16], FINE_LANES, 1))
     fine_copies = []
@@ -546,42 +622,39 @@
     pl.semaphore_wait(ready.at[1], 2)
     announce(2, 2)
 
-    lanes = iota((1, elems), 1)
-    offset = move_dom_ref[...] - d
-    offset = jnp.where(offset < 0, offset + n_dom, offset)
-    chosen = jnp.where(iota((16, elems), 0) == offset, 1.0, 0.0)
-    before = jnp.where(iota((elems, elems), 0) < iota((elems, elems), 1), 1.0, 0.0).astype(BF16)
-    rank = jnp.sum(chosen * dot(chosen.astype(BF16), before), axis=0, keepdims=True)
-    slots = n_dom * MIGRANTS
-    padded = 384 if slots <= 384 else 128 * (-(-slots // 128))
-    position = jnp.where(offset == 0, -1, offset * MIGRANTS + rank.astype(jnp.int32))
-    inverse = jnp.where(iota((padded, elems), 0) == position, 1.0, 0.0).astype(BF16)
-    place = move_slot_ref[...]
-    which_row = iota((8, elems), 0)
-    facts = jnp.where(
-        which_row == 0,
-        lanes >> 1,
-        jnp.where(
-            which_row == 1, lanes & 1, jnp.where(which_row == 2, place >> 1, place & 1)
-        ),
-    )
-    facts = jnp.where(which_row < 4, facts, 0).astype(F32).astype(BF16)
-    found = dot_nt(facts, inverse).astype(jnp.int32)
-    leaves = found[0:1] * 2 + found[1:2]
-    lands = found[2:3] * 2 + found[3:4]
-    for k in range(1, n_dom):
-        land_out[k] = lands[:, 128 * (k // 4) : 128 * (k // 4) + 128]
-
-    tab_c[48:96] = dot(traces[48:96], second_split)
+    for b in range(blocks):
+        columns = slice(128 * b, 128 * b + 128)
+        index = jnp.broadcast_to(fine_rank[:, columns] & 127, (8, 128))
+        mine = jnp.broadcast_to(cluster_ref[:, columns], (8, 128)) == 0
+        for g in range(4):
+            rows = slice(8 * g, 8 * g + 8)
+            found = jnp.take_along_axis(fine[rows], index, axis=1)
+            dense[rows, columns] = jnp.where(mine, found, later[rows, columns])
+    second_split = split_state(dense[...])
+    tab_c[...] = dot(traces, second_split)
     local_part(tab_c)
     wait_recv(late_copies)
-    remote_part(1)
+
+    lane16 = iota((16, 128), 1)
+    both = []
+    for k in range(6):
+        first = early_slot(3 * blocks + k)
+        if k < 4:
+            coarse = in_reg[1, k // 2, k % 2]
+            if k % 2 == 0:
+                coarse = jnp.where(lane16 < REG_FINE, 0.0, coarse)
+        else:
+            coarse = jnp.where(lane16 < DOM_FINE, 0.0, in_dom[1, k - 4])
+        both.append(first + coarse)
     columns = {}
     for f in range(3):
         for b in range(blocks):
-            columns[f, b] = fine_column(code_of(f, b))
-            beyond[f, b] = jnp.where(columns[f, b] >= 0, 0.0, beyond[f, b])
-    dense[...] = midway + increment(second_split, tab_c)
+            code = code_of(f, b)
+            columns[f, b] = fine_column(code)
+            beyond[f, b] = pick_columns(
+                lambda k: both[k - 3 * blocks], remote, code >> 7, code & 127, beyond[f, b]
+            )
+    dense[...] = base[...] + increment(second_split, tab_c)
     pl.semaphore_wait(ready.at[2], 2)
     land_copies = peer_copies(land_out, land_in, ss_land, rs_land)
     for k in nearest[::-1]:
@@ -597,7 +670,7 @@
             jnp.where(at < 2 * REG_FINE + DOM_FINE, in_fine[2], in_fine[3]),
         ),
     )
-    parts = []
+    outer = []
     for f in range(3):
         late = []
         for b in range(blocks):
@@ -606,10 +679,8 @@
             high = jnp.take_along_axis(fresh, column + FINE_LANES, axis=1)
             found = jnp.concatenate([low, high], axis=0)
             late.append(jnp.where(columns[f, b] >= 0, found, 0.0))
-        late = jnp.concatenate(late, axis=1)
-        parts.append(centre_by[f] * late)
-        parts.append(jump_by[f] * late)
-    dense[...] = dense[...] + dot(lift, split_state(jnp.concatenate(parts, axis=0)))
+        outer.append(jnp.concatenate(late, axis=1))
+    dense[...] = dense[...] + lifted(lift, factors, outer, outer)
 
     def cell(g, b):
         return dense[8 * g : 8 * g + 8, 128 * b : 128 * b + 128]
@@ -632,20 +703,7 @@
                 moved = pltpu.roll(moved, shift, 1)
             tile = jnp.where(group == g, moved, tile)
         tile_out[k] = tile
-    for target in range(n_dom):
-
-        @pl.when(target != d)
-        def _():
-            k = lax.rem(target - d + n_dom, n_dom)
-            pltpu.make_async_remote_copy(
-                src_ref=tile_out.at[k],
-                dst_ref=tile_in.at[k],
-                send_sem=ss_tile.at[k],
-                recv_sem=rs_tile.at[k],
-                device_id={"dom": target},
-                device_id_type=MESH,
-            ).start()
-
+        tile_copies[k].start()
     for k in range(1, n_dom):
         land_copies[k].wait_recv()
     kk = iota((1, 128), 1)
@@ -671,8 +729,21 @@
         land_copies[k].wait_send()
         tile_copies[k].wait_send()
     result = {(g, b): cell(g, b) for g in range(4) for b in range(blocks)}
-    for k in nearest:
-        tile_copies[k].wait_recv()
+    half = n_dom // 2
+    for sender in [*range(half), *reversed(range(half, n_dom))]:
+        k = lax.rem(d - sender + n_dom, n_dom)
+
+        @pl.when(sender != d)
+        def _():
+            pltpu.make_async_remote_copy(
+                src_ref=tile_out.at[k],
+                dst_ref=tile_in.at[k],
+                send_sem=ss_tile.at[k],
+                recv_sem=rs_tile.at[k],
+                device_id={"dom": sender},
+                device_id_type=MESH,
+            ).wait_recv()
+
         tile = tile_in[k]
         for b in range(blocks):
             index = jnp.broadcast_to(origin[:, 128 * b : 128 * b + 128], (8, 128))
@@ -740,6 +811,8 @@
             pltpu.VMEM((32, 16), F32),
             pltpu.VMEM((16, 16), F32),
             pltpu.VMEM((32, elems), F32),
+            pltpu.VMEM((32, elems), F32),
+            pltpu.VMEM((8, elems), F32),
             pltpu.VMEM((96, elems), F32),
             pltpu.VMEM((48, elems), F32),
             pltpu.VMEM((96, elems), F32),

time: 30.1 us -> 29.8 us (0.990)
  Pallas kernels: 29.3 us -> 28.9 us
    pallas_call x1, Pallas kernels: 29.3 us -> 28.9 us  [shards(): pl.pallas_call(kernel, out_shape=pltpu.VMEM((NODES, 3, elems), F32), in_s...]
where the time goes in v5:
time: 29.8 us; the launch traced here: 29.6 us
  Pallas kernels  28.9 us (97%)
  local copies, waits for them, and re-layouts  0.64 us (2%)
    pallas_call x1, Pallas kernels, shards(): pl.pallas_call(kernel, out_shape=pltpu.VMEM((NODES, 3, elems), F32), in_s...  28.9 us
    unnamed x1, local copies, waits for them, and re-layouts  0.64 us

profile of v5, /device:TPU:6, one launch (start us, length us, event | category | flops | bytes accessed | tf_op | source)
XLA Modules:
  0.0 29.6 jit_solution(14752512650869562512)
XLA Ops:
  0.0 28.9 %wave_step.1 = f32[10,3,512]{2,1,0:T(4,128)S(1)} custom-call(f32[10,3,512]{2,1,0:T(4,128)} %bitcast.10, f32[1,512]{1,0:T(1,128)} %bitcast.14, f32[4,512]{1,0:T(4,128)} %refs_2_.1, f32[10,2,10]{2,1,0:T(2,128)} %bitcast.11, f32[10,2,10]{2,1,0:T(2,128)} %bitcast.12, f32[3,4,10]{2,1,0:T(4,128)} %refs_5_.1, f32[3,4,10]{2,1,0:T(4,128)} %bitcast.13, ...), custom_call_target="tpu_custom_call" | custom-call | tf_op jit(solution)/shard_map/wave_step/pallas_call | solution.py:801
  29.0 0.6 %copy.21 = f32[3,10,512]{2,0,1:T(4,128)} copy(f32[3,10,512]{2,0,1:T(4,128)S(1)} %bitcast.9) | data formatting | bytes 122880

commit v6 on v5

--- a/solution.py
+++ b/solution.py
@@ -410,7 +410,8 @@
     tab_b[...] = dot(traces[0:48], split_state(later))
     gather_sends(1, tab_b, late_copies)
 
-    tile_in[0] = jnp.zeros((8, 128), F32)
+    tile_in[d] = jnp.zeros((8, 128), F32)
+    land_in[d] = jnp.full((1, 128), -1, jnp.int32)
     for i in range(2):
 
         @pl.when(jnp.logical_not(comes[i]))
@@ -487,28 +488,52 @@
     base[...] = state + increment(early_split, tab_a)
     pl.semaphore_wait(ready.at[0], 2)
     announce(1, 2)
-    nearest = sorted(range(1, n_dom), key=lambda k: min(k, n_dom - k))
-
-    def peer_copies(src, dst, ss, rs):
-        return {
-            k: pltpu.make_async_remote_copy(
-                src_ref=src.at[k],
-                dst_ref=dst.at[k],
-                send_sem=ss.at[k],
-                recv_sem=rs.at[k],
-                device_id={"dom": lax.rem(d + k, n_dom)},
+
+    def to_peers(src, dst, ss, rs):
+        return [
+            pltpu.make_async_remote_copy(
+                src_ref=src.at[t],
+                dst_ref=dst.at[d],
+                send_sem=ss.at[t],
+                recv_sem=rs.at[d],
+                device_id={"dom": t},
                 device_id_type=MESH,
             )
-            for k in range(1, n_dom)
-        }
+            for t in range(n_dom)
+        ]
+
+    def from_peers(src, dst, ss, rs):
+        return [
+            pltpu.make_async_remote_copy(
+                src_ref=src.at[t],
+                dst_ref=dst.at[t],
+                send_sem=ss.at[t],
+                recv_sem=rs.at[t],
+                device_id={"dom": t},
+                device_id_type=MESH,
+            )
+            for t in range(n_dom)
+        ]
+
+    def unless_own(t, action):
+        pl.when(t != d)(action)
+
+    land_copies = to_peers(land_out, land_in, ss_land, rs_land)
+    tile_copies = to_peers(tile_out, tile_in, ss_tile, rs_tile)
+    land_comes = from_peers(land_out, land_in, ss_land, rs_land)
+    tile_comes = from_peers(tile_out, tile_in, ss_tile, rs_tile)
+
+    def within(t, reach):
+        apart = lax.rem(t - d + n_dom, n_dom)
+        return (apart != 0) & ((apart <= reach) | (apart >= n_dom - reach))
 
     lanes = iota((1, elems), 1)
-    offset = move_dom_ref[...] - d
-    offset = jnp.where(offset < 0, offset + n_dom, offset)
+    target = move_dom_ref[...]
+    target = jnp.where(target == d, -1, target)
     fine_row = 15
     is_fine = cluster_ref[...] == 0
     kind = iota((16, elems), 0)
-    chosen = jnp.where(kind == offset, 1.0, 0.0)
+    chosen = jnp.where(kind == target, 1.0, 0.0)
     chosen = jnp.where(kind == fine_row, jnp.where(is_fine, 1.0, 0.0), chosen)
     before = jnp.where(iota((elems, elems), 0) < iota((elems, elems), 1), 1.0, 0.0).astype(BF16)
     ranks = dot(chosen.astype(BF16), before)
@@ -517,7 +542,7 @@
     fine_position = jnp.where(is_fine, fine_rank, -1)
     slots = n_dom * MIGRANTS
     padded = 384 if slots <= 384 else 128 * (-(-slots // 128))
-    position = jnp.where(offset == 0, -1, offset * MIGRANTS + rank.astype(jnp.int32))
+    position = jnp.where(target < 0, -1, target * MIGRANTS + rank.astype(jnp.int32))
     inverse = jnp.concatenate(
         [
             jnp.where(iota((padded, elems), 0) == position, 1.0, 0.0),
@@ -539,8 +564,10 @@
     leaves = found[0:1] * 2 + found[1:2]
     lands = found[2:3] * 2 + found[3:4]
     fine_at = leaves[:, padded : padded + 128]
-    for k in range(1, n_dom):
-        land_out[k] = lands[:, 128 * (k // 4) : 128 * (k // 4) + 128]
+    for t in range(n_dom):
+        row = jnp.broadcast_to(lands[:, 128 * (t // 4) : 128 * (t // 4) + 128], (8, 128))
+        row = jnp.take_along_axis(row, (iota((8, 128), 1) & 31) + 32 * (t & 3), axis=1)
+        land_out[t] = row[0:1]
 
     geometry[0:1] = depth
     geometry[1:5] = metric_ref[...]
@@ -621,6 +648,8 @@
     start(fine_copies)
     pl.semaphore_wait(ready.at[1], 2)
     announce(2, 2)
+    for t in range(n_dom):
+        pl.when(within(t, 4))(land_copies[t].start)
 
     for b in range(blocks):
         columns = slice(128 * b, 128 * b + 128)
@@ -656,9 +685,8 @@
             )
     dense[...] = base[...] + increment(second_split, tab_c)
     pl.semaphore_wait(ready.at[2], 2)
-    land_copies = peer_copies(land_out, land_in, ss_land, rs_land)
-    for k in nearest[::-1]:
-        land_copies[k].start()
+    for t in range(n_dom):
+        pl.when((t != d) & jnp.logical_not(within(t, 4)))(land_copies[t].start)
     wait_recv(fine_copies)
     at = lane8 & (FINE_LANES - 1)
     fresh = jnp.where(
@@ -686,7 +714,6 @@
         return dense[8 * g : 8 * g + 8, 128 * b : 128 * b + 128]
 
     group = iota((8, 128), 1) >> 5
-    tile_copies = peer_copies(tile_out, tile_in, ss_tile, rs_tile)
     packed = {}
     for q in range(padded // 128):
         index = jnp.broadcast_to(leaves[:, 128 * q : 128 * q + 128], (8, 128))
@@ -694,25 +721,24 @@
             packed[g, q] = pick_columns(
                 lambda b: cell(g, b), range(blocks), index >> 7, index & 127, jnp.zeros((8, 128), F32)
             )
-    for k in nearest[::-1]:
+    for t in range(n_dom):
         tile = jnp.zeros((8, 128), F32)
         for g in range(4):
-            shift = (32 * (g - (k & 3))) % 128
-            moved = packed[g, k // 4]
+            shift = (32 * (g - (t & 3))) % 128
+            moved = packed[g, t // 4]
             if shift:
                 moved = pltpu.roll(moved, shift, 1)
             tile = jnp.where(group == g, moved, tile)
-        tile_out[k] = tile
-        tile_copies[k].start()
-    for k in range(1, n_dom):
-        land_copies[k].wait_recv()
+        tile_out[t] = tile
+        unless_own(t, tile_copies[t].start)
+    for t in range(n_dom):
+        unless_own(t, land_comes[t].wait_recv)
     kk = iota((1, 128), 1)
     stack = []
     for q in range(padded // 128):
         row_q = jnp.full((1, 128), -1, jnp.int32)
         for k in range(4 * q, min(4 * q + 4, n_dom)):
-            if k > 0:
-                row_q = jnp.where((kk >> 5) == (k & 3), land_in[k], row_q)
+            row_q = jnp.where((kk >> 5) == (k & 3), land_in[k], row_q)
         stack.append(row_q)
     places = jnp.concatenate(stack, axis=1)
     comes_here = jnp.where(iota((elems, padded), 0) == places, 1.0, 0.0).astype(BF16)
@@ -725,32 +751,26 @@
     wait_send(first_copies)
     wait_send(late_copies)
     wait_send(fine_copies)
-    for k in range(1, n_dom):
-        land_copies[k].wait_send()
-        tile_copies[k].wait_send()
+    for t in range(n_dom):
+        unless_own(t, land_copies[t].wait_send)
+        unless_own(t, tile_copies[t].wait_send)
     result = {(g, b): cell(g, b) for g in range(4) for b in range(blocks)}
-    half = n_dom // 2
-    for sender in [*range(half), *reversed(range(half, n_dom))]:
-        k = lax.rem(d - sender + n_dom, n_dom)
-
-        @pl.when(sender != d)
-        def _():
-            pltpu.make_async_remote_copy(
-                src_ref=tile_out.at[k],
-                dst_ref=tile_in.at[k],
-                send_sem=ss_tile.at[k],
-                recv_sem=rs_tile.at[k],
-                device_id={"dom": sender},
-                device_id_type=MESH,
-            ).wait_recv()
-
-        tile = tile_in[k]
-        for b in range(blocks):
-            index = jnp.broadcast_to(origin[:, 128 * b : 128 * b + 128], (8, 128))
-            here = (index >> 5) == k
-            for g in range(4):
-                found = jnp.take_along_axis(tile, (index & 31) + 32 * g, axis=1)
-                result[g, b] = jnp.where(here, found, result[g, b])
+    for q in range(padded // 128):
+        senders = range(4 * q, min(4 * q + 4, n_dom))
+        for t in senders:
+            unless_own(t, tile_comes[t].wait_recv)
+        for g in range(4):
+            rows = jnp.zeros((8, 128), F32)
+            for t in senders:
+                shift = (32 * ((t & 3) - g)) % 128
+                moved = tile_in[t]
+                if shift:
+                    moved = pltpu.roll(moved, shift, 1)
+                rows = jnp.where(group == (t & 3), moved, rows)
+            for b in range(blocks):
+                index = jnp.broadcast_to(origin[:, 128 * b : 128 * b + 128], (8, 128))
+                found = jnp.take_along_axis(rows, index & 127, axis=1)
+                result[g, b] = jnp.where((index >> 7) == q, found, result[g, b])
     for g in range(4):
         for b in range(blocks):
             dense[8 * g : 8 * g + 8, 128 * b : 128 * b + 128] = result[g, b]

time: 29.8 us -> 29.8 us (level)
  no operation moved by 1% of the time
where the time goes in v6:
time: 29.8 us; the launch traced here: 29.6 us
  Pallas kernels  29 us (97%)
  local copies, waits for them, and re-layouts  0.64 us (2%)
    pallas_call x1, Pallas kernels, shards(): pl.pallas_call(kernel, out_shape=pltpu.VMEM((NODES, 3, elems), F32), in_s...  29 us
    unnamed x1, local copies, waits for them, and re-layouts  0.64 us

profile of v6, /device:TPU:6, one launch (start us, length us, event | category | flops | bytes accessed | tf_op | source)
XLA Modules:
  0.0 29.6 jit_solution(4639013290604844159)
XLA Ops:
  0.0 29.0 %wave_step.1 = f32[10,3,512]{2,1,0:T(4,128)S(1)} custom-call(f32[10,3,512]{2,1,0:T(4,128)} %bitcast.10, f32[1,512]{1,0:T(1,128)} %bitcast.14, f32[4,512]{1,0:T(4,128)} %refs_2_.1, f32[10,2,10]{2,1,0:T(2,128)} %bitcast.11, f32[10,2,10]{2,1,0:T(2,128)} %bitcast.12, f32[3,4,10]{2,1,0:T(4,128)} %refs_5_.1, f32[3,4,10]{2,1,0:T(4,128)} %bitcast.13, ...), custom_call_target="tpu_custom_call" | custom-call | tf_op jit(solution)/shard_map/wave_step/pallas_call | solution.py:821
  29.0 0.6 %copy.21 = f32[3,10,512]{2,0,1:T(4,128)} copy(f32[3,10,512]{2,0,1:T(4,128)S(1)} %bitcast.9) | data formatting | bytes 122880

commit v7 on v6

--- a/solution.py
+++ b/solution.py
@@ -16,8 +16,8 @@
 REG_FINE = 8
 DOM_FINE = 4
 FINE_LANES = 32
-EARLY_LOADS = (3, 5, 13, 14, 15, 0, 1, 2, 9, 10)
-LATE_LOADS = (4, 6, 7, 8, 11, 12, 16, 17, 18)
+EARLY_LOADS = (3, 5, 13, 0, 1, 2, 9, 10)
+LATE_LOADS = (4, 6, 7, 8, 11, 12, 14)
 
 
 def iota(shape, dim):
@@ -83,7 +83,15 @@
                 signs[row, column] = 1.0 if part == var else 0.0
             else:
                 signs[row, column] = -1.0 if part in ((1, 2), (0,), (3,))[var] else 0.0
-    return [jnp.asarray(x, BF16) for x in (pick, mask, columns, nodes, places, signs)]
+    first = np.zeros((416, 128), np.float32)
+    first[0:192, 0:96] = mask
+    first[192:384, 0:32] = pick
+    first[384:416, 0:96] = columns.reshape(32, 96)
+    second = np.zeros((96, 288), np.float32)
+    second[0:32] = places.reshape(32, 288)
+    second[32:64] = signs
+    second[64:96, 0:16] = nodes
+    return [jnp.asarray(x, BF16) for x in (first, second)]
 
 
 def halves(values):
@@ -91,9 +99,11 @@
     return hi, (values - hi.astype(F32)).astype(BF16)
 
 
-def spread_columns(values, columns_ref):
+def spread_columns(values, first_ref):
     hi, lo = halves(values)
-    return (dot(hi, columns_ref[0]) + dot(lo, columns_ref[1])).astype(BF16)
+    return (
+        dot(hi, first_ref[384:400, 0:96]) + dot(lo, first_ref[400:416, 0:96])
+    ).astype(BF16)
 
 
 def combine(slopes, alpha):
@@ -161,12 +171,8 @@
     send_dom_ref,
     move_dom_ref,
     move_slot_ref,
-    pick_ref,
-    mask_ref,
-    columns_ref,
-    nodes_ref,
-    places_ref,
-    signs_ref,
+    first_ref,
+    second_ref,
     out_ref,
     *scratch,
 ):
@@ -184,12 +190,8 @@
         send_dom_ref,
         move_dom_ref,
         move_slot_ref,
-        pick_ref,
-        mask_ref,
-        columns_ref,
-        nodes_ref,
-        places_ref,
-        signs_ref,
+        first_ref,
+        second_ref,
     )
     step_body(
         n_region, n_dom, elems, hbm_refs, out_ref, scratch[: len(hbm_refs)], *scratch[len(hbm_refs) :]
@@ -293,12 +295,8 @@
         send_dom_ref,
         move_dom_ref,
         move_slot_ref,
-        pick_ref,
-        mask_ref,
-        columns_ref,
-        nodes_ref,
-        places_ref,
-        signs_ref,
+        first_ref,
+        second_ref,
     ) = local_refs
     first_ops[...] = jnp.zeros((32, 16), F32)
     second_ops[...] = jnp.zeros((32, 16), F32)
@@ -319,8 +317,8 @@
         first_ops[NODES * a : NODES * (a + 1), 0:NODES] = diff_ref[:, a, :]
     for f in range(3):
         first_ops[2 * NODES + 4 * f : 2 * NODES + 4 * f + 4, 0:NODES] = trace_ref[f]
-    wide = dot(pick_ref[...], spread_columns(first_ops[...], columns_ref)).astype(BF16)
-    wide = wide * mask_ref[...]
+    wide = dot(first_ref[192:384, 0:32], spread_columns(first_ops[...], first_ref)).astype(BF16)
+    wide = wide * first_ref[0:192, 0:96]
     slope, traces = wide[0:96], wide[96:192]
 
     def series_of(values, alpha):
@@ -379,8 +377,8 @@
                     pltpu.make_async_remote_copy(
                         src_ref=(out_reg if regional else out_dom).at[which, lane_row],
                         dst_ref=(in_reg if regional else in_dom).at[which, at],
-                        send_sem=(ss_reg if regional else ss_dom).at[which, at],
-                        recv_sem=(rs_reg if regional else rs_dom).at[which, at],
+                        send_sem=(ss_reg if regional else ss_dom).at[which],
+                        recv_sem=(rs_reg if regional else rs_dom).at[which],
                         device_id=device,
                         device_id_type=MESH,
                     ),
@@ -392,16 +390,42 @@
         for exists, _, copy in copies:
             pl.when(exists)(copy.start)
 
-    def wait_recv(copies):
-        for _, arrives, copy in copies:
-            pl.when(arrives)(copy.wait_recv)
-
-    def wait_send(copies):
-        for exists, _, copy in copies:
-            pl.when(exists)(copy.wait_send)
+    def sizes(src, dst, ss, rs):
+        return pltpu.make_async_remote_copy(
+            src_ref=src,
+            dst_ref=dst,
+            send_sem=ss,
+            recv_sem=rs,
+            device_id=ring(1),
+            device_id_type=MESH,
+        )
+
+    def either(condition, yes, no):
+        pl.when(condition)(yes)
+        pl.when(jnp.logical_not(condition))(no)
+
+    inner = (has_low & has_high, dom_low & dom_high)
+
+    def pairs_a(which):
+        return [
+            (sizes(src.at[which], dst.at[which], *sems), sizes(src.at[which, 0], dst.at[which, 0], *sems))
+            for src, dst, sems in (
+                (out_reg, in_reg, (ss_reg.at[which], rs_reg.at[which])),
+                (out_dom, in_dom, (ss_dom.at[which], rs_dom.at[which])),
+            )
+        ]
+
+    def wait_recv(pairs):
+        for condition, (two, one) in zip(inner, pairs):
+            either(condition, two.wait_recv, one.wait_recv)
+
+    def wait_send(pairs):
+        for condition, (two, one) in zip(inner, pairs):
+            either(condition, two.wait_send, one.wait_send)
 
     first_copies = copies_a(0)
     late_copies = copies_a(1)
+    first_pairs, late_pairs = pairs_a(0), pairs_a(1)
     pl.semaphore_wait(barrier, 2 + has_low.astype(jnp.int32) + has_high.astype(jnp.int32))
     announce(0, 1)
     gather_sends(0, tab_a, first_copies)
@@ -433,14 +457,15 @@
     tab_a[48:96] = dot(traces[48:96], early_split)
     for a in range(2):
         second_ops[NODES * a : NODES * (a + 1), 0:NODES] = stiff_ref[:, a, :]
-    stiff = dot(pick_ref[0:96], spread_columns(second_ops[...], columns_ref)).astype(BF16)
-    stiff = -(stiff * mask_ref[0:96])
+    stiff = dot(first_ref[192:288, 0:32], spread_columns(second_ops[...], first_ref)).astype(BF16)
+    stiff = -(stiff * first_ref[0:96, 0:96])
     for f in range(3):
         lift_ops[4 * f : 4 * f + 4, 0:NODES] = lift_ref[f]
     hi, lo = halves(lift_ops[...])
-    lift = dot(dot_nt(nodes_ref[...], hi).astype(BF16), places_ref[0])
-    lift = lift + dot(dot_nt(nodes_ref[...], lo).astype(BF16), places_ref[1])
-    lift = lift.astype(BF16) * signs_ref[...]
+    nodes = second_ref[64:96, 0:16]
+    lift = dot(dot_nt(nodes, hi).astype(BF16), second_ref[0:16])
+    lift = lift + dot(dot_nt(nodes, lo).astype(BF16), second_ref[16:32])
+    lift = lift.astype(BF16) * second_ref[32:64]
     factors = flux_factors(depth, m0, m1, m2, m3)
     mirror = jnp.where((iota((16, 128), 0) >= 4) & (iota((16, 128), 0) < 12), -1.0, 1.0)
     first_code = 3 * elems
@@ -494,34 +519,19 @@
             pltpu.make_async_remote_copy(
                 src_ref=src.at[t],
                 dst_ref=dst.at[d],
-                send_sem=ss.at[t],
-                recv_sem=rs.at[d],
+                send_sem=ss,
+                recv_sem=rs,
                 device_id={"dom": t},
                 device_id_type=MESH,
             )
             for t in range(n_dom)
         ]
 
-    def from_peers(src, dst, ss, rs):
-        return [
-            pltpu.make_async_remote_copy(
-                src_ref=src.at[t],
-                dst_ref=dst.at[t],
-                send_sem=ss.at[t],
-                recv_sem=rs.at[t],
-                device_id={"dom": t},
-                device_id_type=MESH,
-            )
-            for t in range(n_dom)
-        ]
-
-    def unless_own(t, action):
-        pl.when(t != d)(action)
-
+    others = pl.ds(0, n_dom - 1)
     land_copies = to_peers(land_out, land_in, ss_land, rs_land)
-    tile_copies = to_peers(tile_out, tile_in, ss_tile, rs_tile)
-    land_comes = from_peers(land_out, land_in, ss_land, rs_land)
-    tile_comes = from_peers(tile_out, tile_in, ss_tile, rs_tile)
+    land_all = sizes(land_out.at[others], land_in.at[others], ss_land, rs_land)
+    tile_copies = to_peers(tile_out, tile_in, ss_tile, rs_tile.at[d // 4])
+    tile_all = sizes(tile_out.at[others], tile_in.at[others], ss_tile, rs_tile.at[0])
 
     def within(t, reach):
         apart = lax.rem(t - d + n_dom, n_dom)
@@ -609,7 +619,7 @@
     ).astype(jnp.int32)
     wanted_at = spread(wanted_at[0:1]) & 127
 
-    wait_recv(first_copies)
+    wait_recv(first_pairs)
 
     def early_slot(k):
         k = k - 3 * blocks
@@ -628,7 +638,9 @@
         found = jnp.take_along_axis(fine_table[16 * f : 16 * f + 16], wanted_at, axis=1)
         block = jnp.where(wanted_face == f, found, block)
     lane8 = iota((8, 128), 1)
-    out_fine[...] = jnp.where(lane8 < FINE_LANES, block[0:8], pltpu.roll(block[8:16], FINE_LANES, 1))
+    block = jnp.where(lane8 < FINE_LANES, block[0:8], pltpu.roll(block[8:16], FINE_LANES, 1))
+    out_fine[0] = block
+    out_fine[1] = block
     fine_copies = []
     for i, (exists, device, _, at) in enumerate(sides):
         fine_copies.append(
@@ -636,16 +648,23 @@
                 exists,
                 comes[2 * (i // 2) + at],
                 pltpu.make_async_remote_copy(
-                    src_ref=out_fine,
+                    src_ref=out_fine.at[at],
                     dst_ref=in_fine.at[i],
-                    send_sem=ss_fine.at[i],
-                    recv_sem=rs_fine.at[i],
+                    send_sem=ss_fine.at[i // 2],
+                    recv_sem=rs_fine.at[i // 2],
                     device_id=device,
                     device_id_type=MESH,
                 ),
             )
         )
     start(fine_copies)
+    fine_pairs = [
+        (
+            sizes(out_fine, in_fine.at[pl.ds(2 * i, 2)], ss_fine.at[i], rs_fine.at[i]),
+            sizes(out_fine.at[0], in_fine.at[2 * i], ss_fine.at[i], rs_fine.at[i]),
+        )
+        for i in range(2)
+    ]
     pl.semaphore_wait(ready.at[1], 2)
     announce(2, 2)
     for t in range(n_dom):
@@ -662,7 +681,7 @@
     second_split = split_state(dense[...])
     tab_c[...] = dot(traces, second_split)
     local_part(tab_c)
-    wait_recv(late_copies)
+    wait_recv(late_pairs)
 
     lane16 = iota((16, 128), 1)
     both = []
@@ -687,7 +706,7 @@
     pl.semaphore_wait(ready.at[2], 2)
     for t in range(n_dom):
         pl.when((t != d) & jnp.logical_not(within(t, 4)))(land_copies[t].start)
-    wait_recv(fine_copies)
+    wait_recv(fine_pairs)
     at = lane8 & (FINE_LANES - 1)
     fresh = jnp.where(
         at < REG_FINE,
@@ -730,9 +749,8 @@
                 moved = pltpu.roll(moved, shift, 1)
             tile = jnp.where(group == g, moved, tile)
         tile_out[t] = tile
-        unless_own(t, tile_copies[t].start)
-    for t in range(n_dom):
-        unless_own(t, land_comes[t].wait_recv)
+        pl.when(t != d)(tile_copies[t].start)
+    land_all.wait_recv()
     kk = iota((1, 128), 1)
     stack = []
     for q in range(padded // 128):
@@ -748,17 +766,21 @@
     found = dot_nt(facts.astype(F32).astype(BF16), comes_here).astype(jnp.int32)
     origin = jnp.where(found[2:3] > 0, found[0:1] * 2 + found[1:2], -1)
 
-    wait_send(first_copies)
-    wait_send(late_copies)
-    wait_send(fine_copies)
-    for t in range(n_dom):
-        unless_own(t, land_copies[t].wait_send)
-        unless_own(t, tile_copies[t].wait_send)
+    wait_send(first_pairs)
+    wait_send(late_pairs)
+    wait_send(fine_pairs)
+    land_all.wait_send()
+    tile_all.wait_send()
     result = {(g, b): cell(g, b) for g in range(4) for b in range(blocks)}
     for q in range(padded // 128):
         senders = range(4 * q, min(4 * q + 4, n_dom))
-        for t in senders:
-            unless_own(t, tile_comes[t].wait_recv)
+        if not senders:
+            continue
+        full, short = (
+            sizes(tile_out.at[rows], tile_in.at[rows], ss_tile, rs_tile.at[q])
+            for rows in (pl.ds(4 * q, len(senders)), pl.ds(4 * q, len(senders) - 1))
+        )
+        either(d // 4 == q, short.wait_recv, full.wait_recv)
         for g in range(4):
             rows = jnp.zeros((8, 128), F32)
             for t in senders:
@@ -841,22 +863,22 @@
             pltpu.VMEM((2, 2, 16, 128), F32),
             pltpu.VMEM((2, 2, 2, 16, 128), F32),
             pltpu.VMEM((2, 2, 16, 128), F32),
-            pltpu.VMEM((8, 128), F32),
+            pltpu.VMEM((2, 8, 128), F32),
             pltpu.VMEM((4, 8, 128), F32),
             pltpu.VMEM((n_dom, 1, 128), jnp.int32),
             pltpu.VMEM((n_dom, 1, 128), jnp.int32),
             pltpu.VMEM((n_dom, 8, 128), F32),
             pltpu.VMEM((n_dom, 8, 128), F32),
-            dma((2, 2)),
-            dma((2, 2)),
-            dma((2, 2)),
-            dma((2, 2)),
-            dma((4,)),
-            dma((4,)),
-            dma((n_dom,)),
-            dma((n_dom,)),
-            dma((n_dom,)),
-            dma((n_dom,)),
+            dma((2,)),
+            dma((2,)),
+            dma((2,)),
+            dma((2,)),
+            dma((2,)),
+            dma((2,)),
+            dma,
+            dma,
+            dma,
+            dma((-(-n_dom // 4),)),
         ],
         compiler_params=pltpu.CompilerParams(collective_id=0, has_side_effects=True),
         name="wave_step",

time: 29.8 us -> 29.2 us (0.980)
  Pallas kernels: 29 us -> 28.4 us
    pallas_call x1, Pallas kernels: 29 us -> 28.4 us  [shards(): pl.pallas_call(kernel, out_shape=pltpu.VMEM((NODES, 3, elems), F32), in_s...]
where the time goes in v7:
time: 29.2 us; the launch traced here: 29.1 us
  Pallas kernels  28.4 us (97%)
  local copies, waits for them, and re-layouts  0.64 us (2%)
    pallas_call x1, Pallas kernels, shards(): pl.pallas_call(kernel, out_shape=pltpu.VMEM((NODES, 3, elems), F32), in_s...  28.4 us
    unnamed x1, local copies, waits for them, and re-layouts  0.64 us

profile of v7, /device:TPU:6, one launch (start us, length us, event | category | flops | bytes accessed | tf_op | source)
XLA Modules:
  0.0 29.1 jit_solution(7915809308538067313)
XLA Ops:
  0.0 28.4 %wave_step.1 = f32[10,3,512]{2,1,0:T(4,128)S(1)} custom-call(f32[10,3,512]{2,1,0:T(4,128)} %bitcast.10, f32[1,512]{1,0:T(1,128)} %bitcast.14, f32[4,512]{1,0:T(4,128)} %refs_2_.1, f32[10,2,10]{2,1,0:T(2,128)} %bitcast.11, f32[10,2,10]{2,1,0:T(2,128)} %bitcast.12, f32[3,4,10]{2,1,0:T(4,128)} %refs_5_.1, f32[3,4,10]{2,1,0:T(4,128)} %bitcast.13, ...), custom_call_target="tpu_custom_call" | custom-call | tf_op jit(solution)/shard_map/wave_step/pallas_call | solution.py:843
  28.4 0.6 %copy.17 = f32[3,10,512]{2,0,1:T(4,128)} copy(f32[3,10,512]{2,0,1:T(4,128)S(1)} %bitcast.9) | data formatting | bytes 122880

commit v8 on v7

--- a/solution.py
+++ b/solution.py
@@ -301,17 +301,8 @@
     first_ops[...] = jnp.zeros((32, 16), F32)
     second_ops[...] = jnp.zeros((32, 16), F32)
     lift_ops[...] = jnp.zeros((16, 16), F32)
-    for i in EARLY_LOADS:
+    for i in EARLY_LOADS[:3]:
         loads[i].wait()
-
-    dense[30:32, :] = jnp.zeros((2, elems), F32)
-    for v in range(3):
-        dense[NODES * v : NODES * (v + 1), :] = state_ref[:, v, :]
-    state = dense[...]
-    depth = depth_ref[...]
-    m0, m1, m2, m3 = (metric_ref[i : i + 1, :] for i in range(4))
-
-    alpha = alpha_of(depth, m0, m1, m2, m3)
 
     for a in range(2):
         first_ops[NODES * a : NODES * (a + 1), 0:NODES] = diff_ref[:, a, :]
@@ -320,6 +311,18 @@
     wide = dot(first_ref[192:384, 0:32], spread_columns(first_ops[...], first_ref)).astype(BF16)
     wide = wide * first_ref[0:192, 0:96]
     slope, traces = wide[0:96], wide[96:192]
+
+    for i in EARLY_LOADS[3:]:
+        loads[i].wait()
+
+    dense[30:32, :] = jnp.zeros((2, elems), F32)
+    for v in range(3):
+        dense[NODES * v : NODES * (v + 1), :] = state_ref[:, v, :]
+    state = dense[...]
+    depth = depth_ref[...]
+    m0, m1, m2, m3 = (metric_ref[i : i + 1, :] for i in range(4))
+
+    alpha = alpha_of(depth, m0, m1, m2, m3)
 
     def series_of(values, alpha):
         series = [values]
@@ -703,43 +706,62 @@
                 lambda k: both[k - 3 * blocks], remote, code >> 7, code & 127, beyond[f, b]
             )
     dense[...] = base[...] + increment(second_split, tab_c)
+
+    quarters = range(padded // 128)
+    at_of = [leaves[:, 128 * q : 128 * q + 128] for q in quarters]
+    packed_base = {(g, q): squeeze(block_of(dense, g), at_of[q]) for q in quarters for g in range(4)}
+    packed_facts = [squeeze(block_of(geometry, 0), at_of[q]) for q in quarters]
+    packed_factors = flux_factors(
+        *(jnp.concatenate([facts[i : i + 1] for facts in packed_facts], axis=1) for i in range(5))
+    )
+    packed_columns = {
+        (f, q): fine_column(spread(packed_facts[q][5 + f : 6 + f].astype(jnp.int32)))
+        for f in range(3)
+        for q in quarters
+    }
     pl.semaphore_wait(ready.at[2], 2)
     for t in range(n_dom):
         pl.when((t != d) & jnp.logical_not(within(t, 4)))(land_copies[t].start)
     wait_recv(fine_pairs)
     at = lane8 & (FINE_LANES - 1)
-    fresh = jnp.where(
-        at < REG_FINE,
-        in_fine[0],
-        jnp.where(
-            at < 2 * REG_FINE,
-            in_fine[1],
-            jnp.where(at < 2 * REG_FINE + DOM_FINE, in_fine[2], in_fine[3]),
-        ),
-    )
-    outer = []
-    for f in range(3):
-        late = []
-        for b in range(blocks):
-            column = columns[f, b][0:8] & (FINE_LANES - 1)
-            low = jnp.take_along_axis(fresh, column, axis=1)
-            high = jnp.take_along_axis(fresh, column + FINE_LANES, axis=1)
-            found = jnp.concatenate([low, high], axis=0)
-            late.append(jnp.where(columns[f, b] >= 0, found, 0.0))
-        outer.append(jnp.concatenate(late, axis=1))
-    dense[...] = dense[...] + lifted(lift, factors, outer, outer)
+
+    def fine_block():
+        return jnp.where(
+            at < REG_FINE,
+            in_fine[0],
+            jnp.where(
+                at < 2 * REG_FINE,
+                in_fine[1],
+                jnp.where(at < 2 * REG_FINE + DOM_FINE, in_fine[2], in_fine[3]),
+            ),
+        )
+
+    def fine_outer(columns, count):
+        fresh = fine_block()
+        outer = []
+        for f in range(3):
+            late = []
+            for b in range(count):
+                column = columns[f, b][0:8] & (FINE_LANES - 1)
+                low = jnp.take_along_axis(fresh, column, axis=1)
+                high = jnp.take_along_axis(fresh, column + FINE_LANES, axis=1)
+                found = jnp.concatenate([low, high], axis=0)
+                late.append(jnp.where(columns[f, b] >= 0, found, 0.0))
+            outer.append(jnp.concatenate(late, axis=1))
+        return outer
+
+    outer = fine_outer(packed_columns, len(quarters))
+    share = lifted(lift, packed_factors, outer, outer)
 
     def cell(g, b):
         return dense[8 * g : 8 * g + 8, 128 * b : 128 * b + 128]
 
     group = iota((8, 128), 1) >> 5
-    packed = {}
-    for q in range(padded // 128):
-        index = jnp.broadcast_to(leaves[:, 128 * q : 128 * q + 128], (8, 128))
-        for g in range(4):
-            packed[g, q] = pick_columns(
-                lambda b: cell(g, b), range(blocks), index >> 7, index & 127, jnp.zeros((8, 128), F32)
-            )
+    packed = {
+        (g, q): packed_base[g, q] + share[8 * g : 8 * g + 8, 128 * q : 128 * q + 128]
+        for q in quarters
+        for g in range(4)
+    }
     for t in range(n_dom):
         tile = jnp.zeros((8, 128), F32)
         for g in range(4):
@@ -750,6 +772,13 @@
             tile = jnp.where(group == g, moved, tile)
         tile_out[t] = tile
         pl.when(t != d)(tile_copies[t].start)
+    wait_send(first_pairs)
+    wait_send(late_pairs)
+    wait_send(fine_pairs)
+    land_all.wait_send()
+    tile_all.wait_send()
+    outer = fine_outer(columns, blocks)
+    dense[...] = dense[...] + lifted(lift, factors, outer, outer)
     land_all.wait_recv()
     kk = iota((1, 128), 1)
     stack = []
@@ -766,11 +795,6 @@
     found = dot_nt(facts.astype(F32).astype(BF16), comes_here).astype(jnp.int32)
     origin = jnp.where(found[2:3] > 0, found[0:1] * 2 + found[1:2], -1)
 
-    wait_send(first_pairs)
-    wait_send(late_pairs)
-    wait_send(fine_pairs)
-    land_all.wait_send()
-    tile_all.wait_send()
     result = {(g, b): cell(g, b) for g in range(4) for b in range(blocks)}
     for q in range(padded // 128):
         senders = range(4 * q, min(4 * q + 4, n_dom))

time: 29.2 us -> 29.1 us (level)
  no operation moved by 1% of the time
where the time goes in v8:
time: 29.1 us; the launch traced here: 29 us
  Pallas kernels  28.3 us (97%)
  local copies, waits for them, and re-layouts  0.64 us (2%)
    pallas_call x1, Pallas kernels, shards(): pl.pallas_call(kernel, out_shape=pltpu.VMEM((NODES, 3, elems), F32), in_s...  28.3 us
    unnamed x1, local copies, waits for them, and re-layouts  0.64 us

profile of v8, /device:TPU:6, one launch (start us, length us, event | category | flops | bytes accessed | tf_op | source)
XLA Modules:
  0.0 29.0 jit_solution(3106826082004423045)
XLA Ops:
  0.0 28.3 %wave_step.1 = f32[10,3,512]{2,1,0:T(4,128)S(1)} custom-call(f32[10,3,512]{2,1,0:T(4,128)} %bitcast.10, f32[1,512]{1,0:T(1,128)} %bitcast.14, f32[4,512]{1,0:T(4,128)} %refs_2_.1, f32[10,2,10]{2,1,0:T(2,128)} %bitcast.11, f32[10,2,10]{2,1,0:T(2,128)} %bitcast.12, f32[3,4,10]{2,1,0:T(4,128)} %refs_5_.1, f32[3,4,10]{2,1,0:T(4,128)} %bitcast.13, ...), custom_call_target="tpu_custom_call" | custom-call | tf_op jit(solution)/shard_map/wave_step/pallas_call | solution.py:867
  28.3 0.6 %copy.17 = f32[3,10,512]{2,0,1:T(4,128)} copy(f32[3,10,512]{2,0,1:T(4,128)S(1)} %bitcast.9) | data formatting | bytes 122880

commit v9 on v8

--- a/solution.py
+++ b/solution.py
@@ -301,7 +301,7 @@
     first_ops[...] = jnp.zeros((32, 16), F32)
     second_ops[...] = jnp.zeros((32, 16), F32)
     lift_ops[...] = jnp.zeros((16, 16), F32)
-    for i in EARLY_LOADS[:3]:
+    for i in EARLY_LOADS:
         loads[i].wait()
 
     for a in range(2):
@@ -312,9 +312,6 @@
     wide = wide * first_ref[0:192, 0:96]
     slope, traces = wide[0:96], wide[96:192]
 
-    for i in EARLY_LOADS[3:]:
-        loads[i].wait()
-
     dense[30:32, :] = jnp.zeros((2, elems), F32)
     for v in range(3):
         dense[NODES * v : NODES * (v + 1), :] = state_ref[:, v, :]
@@ -353,21 +350,37 @@
 
     own = range(3 * blocks)
 
+    odd = lax.rem(r, 2)
+    far_low, near_low = odd == 0, odd == 1
+
     def gather_sends(which, table, copies):
-        for i, (exists, _, copy) in enumerate(copies):
-            lane_row = sides[i][2]
-            if i < 2:
-                for b in range(2):
-                    index = spread(send_reg_ref[lane_row : lane_row + 1, 128 * b : 128 * b + 128])
-                    out_reg[which, lane_row, b] = pick_columns(
-                        source(table), own, index >> 7, index & 127, jnp.zeros((16, 128), F32)
-                    )
-            else:
-                index = spread(send_dom_ref[lane_row : lane_row + 1, :])
-                out_dom[which, lane_row] = pick_columns(
+        def regional_list(lane_row):
+            for b in range(2):
+                columns = slice(128 * b, 128 * b + 128)
+                index = jnp.where(lane_row == 1, send_reg_ref[1:2, columns], send_reg_ref[0:1, columns])
+                index = spread(index)
+                out_reg[which, lane_row, b] = pick_columns(
                     source(table), own, index >> 7, index & 127, jnp.zeros((16, 128), F32)
                 )
+
+        def leave(i, condition):
+            exists, _, copy = copies[i]
+            pl.when(exists & condition)(copy.start)
+
+        regional_list(odd)
+        leave(1, far_low)
+        leave(0, near_low)
+        for i in (2, 3):
+            exists, _, copy = copies[i]
+            lane_row = sides[i][2]
+            index = spread(send_dom_ref[lane_row : lane_row + 1, :])
+            out_dom[which, lane_row] = pick_columns(
+                source(table), own, index >> 7, index & 127, jnp.zeros((16, 128), F32)
+            )
             pl.when(exists)(copy.start)
+        regional_list(1 - odd)
+        leave(0, far_low)
+        leave(1, near_low)
 
     def copies_a(which):
         copies = []

time: 29.1 us -> 29 us (level)
  no operation moved by 1% of the time
where the time goes in v9:
time: 29 us; the launch traced here: 28.8 us
  Pallas kernels  28.2 us (97%)
  local copies, waits for them, and re-layouts  0.64 us (2%)
    pallas_call x1, Pallas kernels, shards(): pl.pallas_call(kernel, out_shape=pltpu.VMEM((NODES, 3, elems), F32), in_s...  28.2 us
    unnamed x1, local copies, waits for them, and re-layouts  0.64 us

profile of v9, /device:TPU:6, one launch (start us, length us, event | category | flops | bytes accessed | tf_op | source)
XLA Modules:
  0.0 28.8 jit_solution(11459763662394633239)
XLA Ops:
  0.0 28.2 %wave_step.1 = f32[10,3,512]{2,1,0:T(4,128)S(1)} custom-call(f32[10,3,512]{2,1,0:T(4,128)} %bitcast.10, f32[1,512]{1,0:T(1,128)} %bitcast.14, f32[4,512]{1,0:T(4,128)} %refs_2_.1, f32[10,2,10]{2,1,0:T(2,128)} %bitcast.11, f32[10,2,10]{2,1,0:T(2,128)} %bitcast.12, f32[3,4,10]{2,1,0:T(4,128)} %refs_5_.1, f32[3,4,10]{2,1,0:T(4,128)} %bitcast.13, ...), custom_call_target="tpu_custom_call" | custom-call | tf_op jit(solution)/shard_map/wave_step/pallas_call | solution.py:880
  28.2 0.6 %copy.17 = f32[3,10,512]{2,0,1:T(4,128)} copy(f32[3,10,512]{2,0,1:T(4,128)S(1)} %bitcast.9) | data formatting | bytes 122880

commit v10 on v9

--- a/solution.py
+++ b/solution.py
@@ -262,8 +262,6 @@
     def ring(k):
         return {"dom": lax.rem(d + k + n_dom, n_dom)}
 
-    for i in EARLY_LOADS:
-        loads[i].start()
     for exists, device, _, _ in sides[:2]:
 
         @pl.when(exists)
@@ -272,6 +270,8 @@
 
     for k in (1, -1):
         pl.semaphore_signal(barrier, inc=1, device_id=ring(k), device_id_type=MESH)
+    for i in EARLY_LOADS:
+        loads[i].start()
     for i in LATE_LOADS:
         loads[i].start()
 

time: 29 us -> 28.9 us (level)
  no operation moved by 1% of the time
where the time goes in v10:
time: 28.9 us; the launch traced here: 28.7 us
  Pallas kernels  28.1 us (97%)
  local copies, waits for them, and re-layouts  0.64 us (2%)
    pallas_call x1, Pallas kernels, shards(): pl.pallas_call(kernel, out_shape=pltpu.VMEM((NODES, 3, elems), F32), in_s...  28.1 us
    unnamed x1, local copies, waits for them, and re-layouts  0.64 us

profile of v10, /device:TPU:6, one launch (start us, length us, event | category | flops | bytes accessed | tf_op | source)
XLA Modules:
  0.0 28.7 jit_solution(1769231842267741770)
XLA Ops:
  0.0 28.1 %wave_step.1 = f32[10,3,512]{2,1,0:T(4,128)S(1)} custom-call(f32[10,3,512]{2,1,0:T(4,128)} %bitcast.10, f32[1,512]{1,0:T(1,128)} %bitcast.14, f32[4,512]{1,0:T(4,128)} %refs_2_.1, f32[10,2,10]{2,1,0:T(2,128)} %bitcast.11, f32[10,2,10]{2,1,0:T(2,128)} %bitcast.12, f32[3,4,10]{2,1,0:T(4,128)} %refs_5_.1, f32[3,4,10]{2,1,0:T(4,128)} %bitcast.13, ...), custom_call_target="tpu_custom_call" | custom-call | tf_op jit(solution)/shard_map/wave_step/pallas_call | solution.py:880
  28.1 0.6 %copy.17 = f32[3,10,512]{2,0,1:T(4,128)} copy(f32[3,10,512]{2,0,1:T(4,128)S(1)} %bitcast.9) | data formatting | bytes 122880
